TPU v7x, 32 devices: a whole 2x2x4 slice. The times are simulated.
32 devices in a mesh: dom: 16 (over z, y, x), spin: 2 (over core).
Axes of the slice: x: 2, y: 2, z: 4, core: 2. Of those that a mesh axis runs over, the one named last changes fastest.
Arguments:
- vectors: float32 [2, 8, 262144], P('spin', None, 'dom'), may hold values from -17 to 17
- basis: float32 [2, 16, 262144], P('spin', None, 'dom'), may hold values from -17 to 17
- potential: float32 [2, 262144], P('spin', 'dom'), may hold values from 1 to 3
- hop_table: bfloat16 [8, 128, 128], replicated, may hold values from -0.25 to 0.25
- soc_table: bfloat16 [2, 128, 128], replicated, may hold values from -0.5 to 0.5
- nbr_block: int32 [2048, 16], P('dom'), may hold values from 0 to 2047, as said below
- nbr_type: int32 [2048, 16], P('dom'), may hold values from 0 to 7
- nbr_count: int32 [2048], P('dom'), may hold values from 1 to 16, as said below
- flip_block: int32 [2048], P('dom'), may hold values from 0 to 2047, as said below
Outputs:
- block_one: float32 [2, 8, 262144], P('spin', None, 'dom')
- block_two: float32 [2, 8, 262144], P('spin', None, 'dom')
- coefs_one: float32 [32, 8], replicated
- coefs_two: float32 [40, 8], replicated
Inputs may be any that keep to these rules, and one draw needn't show every extreme that they name: nbr_block[i, l] equals i + d modulo 2048 with -8 <= d <= 8; slots at or beyond nbr_count[i] are ignored; in slot 0, the first block of each group of 128 has d = -8 and the last has d = 8. `nbr_count`: some block has all 16 slots live. flip_block[i] lies in the same domain as i: flip_block[i] // 128 == i // 128.
All inputs are finite; a program needn't handle non-finite values.
Results may differ from a plain program's by a relative error of at most 0.0033.
Values may be sent and summed in bfloat16 or wider, within the bound.
A program may use at most 64 MiB of HBM per device.

v0:
```python
import functools
import jax
import jax.numpy as jnp
from jax import lax
from jax.experimental import pallas as pl
from jax.experimental.pallas import tpu as pltpu
from jax.sharding import PartitionSpec as P

RANGE = 8
MESH = pl.DeviceIdType.MESH
NT = (((1,), (1,)), ((), ()))
NN = (((1,), (0,)), ((), ()))


def high_dot(left, right, dims):
    return lax.dot_general(
        left, right, dims, precision=lax.Precision.HIGHEST, preferred_element_type=jnp.float32
    )


def spread(table, bcast_ref, count, vecs, width):
    for m in range(count):
        bcast_ref[m] = jnp.broadcast_to(table[:, vecs + m:vecs + m + 1], (vecs, width))


def combine(work_ref, bcast_ref, image_row, span_rows, vecs, width, out_ref, ext_out):
    step = 4
    order = [image_row + r for r in range(vecs)] + span_rows

    def cols(tile):
        return pl.ds(pl.multiple_of(tile * width, width), width)

    def body(chunk, carry):
        sums = [None] * step
        for m, r in enumerate(order):
            coef = bcast_ref[m]
            for u in range(step):
                term = coef * work_ref[pl.ds(r, 1), cols(chunk * step + u)]
                sums[u] = term if sums[u] is None else sums[u] + term
        for u in range(step):
            out_ref[:, cols(chunk * step + u)] = sums[u]
        if ext_out is not None:
            for u in range(0, step, 2):
                pair = jnp.concatenate(sums[u:u + 2], axis=0).astype(jnp.bfloat16)
                at = pl.multiple_of((chunk * step + u) * vecs, 2 * vecs)
                ext_out[pl.ds(at, 2 * vecs), :] = pair
        return carry
    return step, body


def kernel(
    cfg,
    vec_hbm, basis_hbm, pot_hbm, hop_hbm, soc_hbm, nbr_hbm, type_hbm, count_hbm, flip_hbm,
    one_hbm, image_hbm, small_ref,
    work_ref, bcast_ref, pot_ref, hop_ref, soc_ref, nbr_ref, type_ref, count_ref, fliploc_ref, table_ref, idx_ref,
    ext_ref, other_ref, halo_ref, prod_ref, stage_a_ref, stage_b_ref,
    load_sem, link_send, link_recv, a_send, a_recv, b_send, b_recv,
):
    dom_total, group_doms, blocks, width, types, slots, vecs, kept, norm = cfg
    span_one = kept + vecs
    span_two = span_one + vecs
    loads = [
        pltpu.make_async_copy(src, dst, load_sem.at[n])
        for n, (src, dst) in enumerate([
            (nbr_hbm, nbr_ref), (type_hbm, type_ref), (count_hbm, count_ref),
            (flip_hbm, fliploc_ref), (vec_hbm.at[0], work_ref.at[pl.ds(kept, vecs)]),
            (basis_hbm.at[0], work_ref.at[pl.ds(0, kept)]), (hop_hbm, hop_ref),
            (pot_hbm, pot_ref), (soc_hbm, soc_ref)])
    ]
    for copy in loads:
        copy.start()
    table_copy = pltpu.make_async_copy(table_ref, idx_ref, load_sem.at[len(loads)])
    groups = dom_total // group_doms
    group_size = 2 * group_doms
    dom, spin = lax.axis_index("dom"), lax.axis_index("spin")
    rank_a = (dom % group_doms) * 2 + spin
    rank_b = dom // group_doms
    dom_base = rank_b * group_doms
    left, right = (dom + dom_total - 1) % dom_total, (dom + 1) % dom_total
    rows = blocks * vecs
    halo_rows = RANGE * vecs
    reach = blocks + 2 * RANGE
    zero_tile = reach * types
    flip_base = zero_tile + 1

    def peer_a(shift):
        other = (rank_a + shift) % group_size
        return (dom_base + other // 2, other % 2)

    def peer_b(shift):
        return (((rank_b + shift) % groups) * group_doms + dom % group_doms, spin)

    barrier = pltpu.get_barrier_semaphore()
    for shift in range(1, group_size):
        pl.semaphore_signal(barrier, inc=1, device_id=peer_a(shift), device_id_type=MESH)
    for shift in range(1, groups):
        pl.semaphore_signal(barrier, inc=1, device_id=peer_b(shift), device_id_type=MESH)
    for side in (left, right):
        pl.semaphore_signal(barrier, inc=1, device_id=(side, spin), device_id_type=MESH)

    lane = lax.broadcasted_iota(jnp.int32, (vecs, width), 1)
    row = lax.broadcasted_iota(jnp.int32, (vecs, width), 0)

    def cols(tile):
        return pl.ds(pl.multiple_of(tile * width, width), width)

    def link_copies(app):
        ext, halo = ext_ref.at[app], halo_ref.at[app]
        tail = pltpu.make_async_remote_copy(
            src_ref=ext.at[pl.ds(rows - halo_rows, halo_rows)],
            dst_ref=halo.at[pl.ds(0, halo_rows)],
            send_sem=link_send.at[app, 0], recv_sem=link_recv.at[app, 0],
            device_id=(right, spin), device_id_type=MESH)
        head = pltpu.make_async_remote_copy(
            src_ref=ext.at[pl.ds(0, halo_rows)],
            dst_ref=halo.at[pl.ds(halo_rows, halo_rows)],
            send_sem=link_send.at[app, 1], recv_sem=link_recv.at[app, 1],
            device_id=(left, spin), device_id_type=MESH)
        flip = pltpu.make_async_remote_copy(
            src_ref=ext, dst_ref=other_ref.at[app],
            send_sem=link_send.at[app, 2], recv_sem=link_recv.at[app, 2],
            device_id=(dom, 1 - spin), device_id_type=MESH)
        return tail, head, flip

    def gram_rows(left_ref, sources):
        count = sum(hi for _, hi in sources)

        def body(tile, sums):
            ours = left_ref[:, cols(tile)]
            picked = [ref[pl.ds(m, 1), cols(tile)] for ref, hi in sources for m in range(hi)]
            return tuple(total + ours * one for total, one in zip(sums, picked))

        sums = lax.fori_loop(
            0, blocks, body, tuple(jnp.zeros((vecs, width), jnp.float32) for _ in range(count)),
            unroll=2)
        out = jnp.zeros((vecs, width), jnp.float32)
        for m, total in enumerate(sums):
            out = jnp.where(lane == m, jnp.sum(total, axis=1, keepdims=True), out)
        return out

    def products(source, count, first):
        def body(pair, carry):
            weights = hop_ref[pl.ds(pl.multiple_of(pair * 2 * width, 2 * width), 2 * width), :]
            out = lax.dot_general(source[...], weights, NT, preferred_element_type=jnp.float32)
            for half in range(2):
                part = out[:, half * width:(half + 1) * width].reshape(count, vecs, width)
                prod_ref[pl.ds((pair * 2 + half) * reach + first, count)] = part
            return carry
        lax.fori_loop(0, types // 2, body, 0)

    def flip_products(app):
        out = lax.dot_general(
            other_ref[app], soc_ref[spin], NT, preferred_element_type=jnp.float32)
        prod_ref[pl.ds(flip_base, blocks)] = out.reshape(blocks, vecs, width)

    def gather(field_ref, low, high):
        def body(block, carry):
            terms = [pot_ref[pl.ds(0, 1), cols(block)] * field_ref[:, cols(block)]]
            for slot in range(slots + 1):
                terms.append(prod_ref[idx_ref[block, slot]])
            while len(terms) > 1:
                terms = [sum(terms[p:p + 2][1:], terms[p]) for p in range(0, len(terms), 2)]
            image_ref[:, cols(block)] = terms[0]
            return carry
        lax.fori_loop(low, high, body, 0, unroll=2)

    def share(app, value):
        def stage(ref, send, recv, rank, size, peer, mine):
            ref[app, rank] = mine
            def copy(shift, slot):
                return pltpu.make_async_remote_copy(
                    src_ref=ref.at[app, rank], dst_ref=ref.at[app, slot],
                    send_sem=send.at[app, shift], recv_sem=recv.at[app, slot],
                    device_id=peer(shift), device_id_type=MESH)
            for shift in range(1, size):
                copy(shift, rank).start()
            for shift in range(1, size):
                copy(shift, (rank + size - shift) % size).wait_recv()
            for shift in range(1, size):
                copy(shift, rank).wait_send()
            total = ref[app, 0]
            for slot in range(1, size):
                total = total + ref[app, slot]
            return total
        value = stage(stage_a_ref, a_send, a_recv, rank_a, group_size, peer_a, value)
        if groups > 1:
            value = stage(stage_b_ref, b_send, b_recv, rank_b, groups, peer_b, value)
        return value * (1.0 / norm)

    def lanes(value, start, count):
        moved = value if start == 0 else pltpu.roll(value, width - start, 1)
        return jnp.where(lane < count, moved, 0.0)

    def tall(pieces):
        pad = width - vecs * len(pieces)
        return jnp.concatenate(list(pieces) + [jnp.zeros((pad, width), jnp.float32)], axis=0)

    def factor(first_t, image_gram, span_gram, span_count):
        total_t = 2.0 * first_t - high_dot(first_t, span_gram, NT)
        moved = high_dot(total_t, span_gram, NT) - first_t
        gram = image_gram + high_dot(moved, tall([total_t]), NT) - high_dot(total_t, tall([first_t]), NT)
        table = jnp.where(lane < vecs, gram, jnp.where(lane == row + vecs, 1.0, 0.0))
        table = table - pltpu.roll(total_t, 2 * vecs, 1)
        lower = jnp.zeros((vecs, width), jnp.float32)
        for j in range(vecs):
            column = jnp.broadcast_to(table[:, j:j + 1], (vecs, width))
            pivot_row = jnp.broadcast_to(table[j:j + 1, :], (vecs, width))
            pivot = jnp.broadcast_to(column[j:j + 1, :], (vecs, width))
            scale = 1.0 / jnp.sqrt(pivot)
            lower = jnp.where((lane == j) & (row >= j), column * scale, lower)
            pivot_row = pivot_row * scale
            table = jnp.where(
                row == j, pivot_row, jnp.where(row > j, table - column * scale * pivot_row, table))
        return total_t + pltpu.roll(lower, span_count, 1), table

    basis = work_ref.at[pl.ds(0, kept)]
    field = work_ref.at[pl.ds(kept, vecs)]
    one = work_ref.at[pl.ds(span_one, vecs)]
    image_ref = work_ref.at[pl.ds(span_two, vecs)]

    for copy in loads[:4]:
        copy.wait()
    local = lax.broadcasted_iota(jnp.int32, (slots, blocks), 1)
    slot_at = lax.broadcasted_iota(jnp.int32, (slots, blocks), 0)
    shift = nbr_ref[...] - (dom * blocks + local) + RANGE
    total = dom_total * blocks
    shift = jnp.where(shift < 0, shift + total, shift)
    shift = jnp.where(shift >= total, shift - total, shift)
    place = local + shift - RANGE
    place = jnp.where(
        place < 0, place + blocks + RANGE, jnp.where(place >= blocks, place + RANGE, place))
    live = slot_at < count_ref[...]
    index = jnp.concatenate([
        jnp.where(live, type_ref[...] * reach + place, zero_tile),
        jnp.broadcast_to(fliploc_ref[...] - dom * blocks + flip_base, (8, blocks)),
        jnp.zeros((width - slots - 8, blocks), jnp.int32)], axis=0)
    table_ref[...] = jnp.clip(index, 0, flip_base + blocks - 1).T
    table_copy.start()
    loads[4].wait()

    def round_body(pair, carry):
        both = jnp.concatenate([field[:, cols(2 * pair)], field[:, cols(2 * pair + 1)]], axis=0)
        ext_ref[0, pl.ds(pl.multiple_of(pair * 2 * vecs, 2 * vecs), 2 * vecs), :] = both.astype(
            jnp.bfloat16)
        return carry

    lax.fori_loop(0, blocks // 2, round_body, 0, unroll=4)
    prod_ref[zero_tile] = jnp.zeros((vecs, width), jnp.float32)
    loads[5].wait()
    low_gram = [gram_rows(basis.at[pl.ds(g * vecs, vecs)], [(basis, (g + 1) * vecs)])
                for g in range(kept // vecs)]
    low_gram.append(gram_rows(field, [(basis, kept), (field, vecs)]))
    for copy in loads[6:] + [table_copy]:
        copy.wait()
    pl.semaphore_wait(barrier, group_size - 1 + groups - 1 + 2)

    def apply_and_gram(app, field_ref, extra, sources):
        tail, head, flip = link_copies(app)
        products(ext_ref.at[app], blocks, 0)
        early = extra()
        flip.wait_recv()
        flip_products(app)
        gather(field_ref, RANGE, blocks - RANGE)
        tail.wait_recv()
        head.wait_recv()
        products(halo_ref.at[app], 2 * RANGE, blocks)
        gather(field_ref, 0, RANGE)
        gather(field_ref, blocks - RANGE, blocks)
        result = gram_rows(image_ref, sources + [(image_ref, vecs)])
        tail.wait_send()
        head.wait_send()
        flip.wait_send()
        return result, early

    for copy in link_copies(0):
        copy.start()
    result, _ = apply_and_gram(0, field, lambda: None, [(basis, kept), (field, vecs)])
    packed = result
    at = span_one + vecs
    for g in range(span_one // vecs):
        packed = packed + pltpu.roll(low_gram[g], at, 1)
        at += (g + 1) * vecs
    packed = share(0, packed)
    pieces = []
    at = span_one + vecs
    for g in range(span_one // vecs):
        pieces.append(lanes(packed, at, (g + 1) * vecs))
        at += (g + 1) * vecs
    low = tall(pieces)
    wide_row = lax.broadcasted_iota(jnp.int32, (width, width), 0) // vecs
    wide_lane = lax.broadcasted_iota(jnp.int32, (width, width), 1) // vecs
    span_gram = low + jnp.where(wide_row < wide_lane, low.T, 0.0)
    coefs, table = factor(
        lanes(packed, 0, span_one), lanes(packed, span_one, vecs), span_gram, span_one)
    small_ref[pl.ds(0, vecs), :] = coefs
    spread(table, bcast_ref, vecs + span_one, vecs, width)

    step, body = combine(
        work_ref, bcast_ref, span_two, list(range(span_one)), vecs, width, one, ext_ref.at[1])
    chunks, edge = blocks // step, RANGE // step
    tail, head, flip = link_copies(1)
    lax.fori_loop(0, edge, body, 0)
    lax.fori_loop(chunks - edge, chunks, body, 0)
    tail.start()
    head.start()
    lax.fori_loop(edge, chunks - edge, body, 0)
    flip.start()
    one_out = pltpu.make_async_copy(
        work_ref.at[pl.ds(span_one, vecs)], one_hbm, load_sem.at[len(loads) + 1])
    one_out.start()

    result, early = apply_and_gram(
        1, one,
        lambda: gram_rows(one, [(basis, kept), (field, vecs), (one, vecs)]),
        [(basis, kept), (field, vecs), (one, vecs)])
    image_out = pltpu.make_async_copy(
        work_ref.at[pl.ds(span_two, vecs)], image_hbm, load_sem.at[len(loads) + 2])
    image_out.start()
    packed = share(1, result + pltpu.roll(early, 64, 1))
    low = jnp.concatenate(
        [jnp.zeros((span_one, width), jnp.float32), lanes(packed, 64, span_two),
         jnp.zeros((width - span_two, width), jnp.float32)], axis=0)
    span_gram = span_gram + low + jnp.where(wide_row < wide_lane, low.T, 0.0)
    coefs, table = factor(
        lanes(packed, 0, span_two), lanes(packed, span_two, vecs), span_gram, span_two)
    small_ref[pl.ds(vecs, vecs), :] = coefs
    small_ref[pl.ds(2 * vecs, vecs), :] = table
    one_out.wait()
    image_out.wait()


def finish(
    cfg, small_ref, vec_hbm, basis_hbm, one_in_hbm, image_hbm,
    one_hbm, two_hbm, coef_one_hbm, coef_two_hbm,
    work_ref, bcast_ref, two_ref, cut_one_ref, cut_two_ref, load_sem, store_sem,
):
    _, _, blocks, width, _, _, vecs, kept, _ = cfg
    span_one = kept + vecs
    span_two = span_one + vecs
    pieces = 4
    step = 4
    chunks = blocks // step // pieces
    span = chunks * step * width
    loads = []
    for piece in range(pieces):
        part = pl.ds(piece * span, span)
        for n, (src, start, count) in enumerate([
            (basis_hbm.at[0], 0, kept), (vec_hbm.at[0], kept, vecs),
            (one_in_hbm, span_one, vecs), (image_hbm, span_two, vecs)]):
            loads.append(pltpu.make_async_copy(
                src.at[:, part], work_ref.at[pl.ds(start, count), part], load_sem.at[piece, n]))
            loads[-1].start()
    cut_one_ref[...] = small_ref[pl.ds(0, vecs), :span_one + vecs]
    cut_two_ref[...] = small_ref[pl.ds(vecs, vecs), :span_two + vecs]
    stores = [
        pltpu.make_async_copy(cut_one_ref, coef_one_hbm, store_sem.at[0]),
        pltpu.make_async_copy(cut_two_ref, coef_two_hbm, store_sem.at[1])]
    for copy in stores:
        copy.start()
    spread(small_ref[pl.ds(2 * vecs, vecs), :], bcast_ref, vecs + span_two, vecs, width)
    step, body = combine(
        work_ref, bcast_ref, span_two, list(range(span_two)), vecs, width, two_ref, None)
    for piece in range(pieces):
        part = pl.ds(piece * span, span)
        for copy in loads[4 * piece:4 * piece + 4]:
            copy.wait()
        stores.append(pltpu.make_async_copy(
            work_ref.at[pl.ds(span_one, vecs), part], one_hbm.at[0, :, part],
            store_sem.at[2 + piece]))
        stores[-1].start()
        lax.fori_loop(piece * chunks, (piece + 1) * chunks, body, 0)
        stores.append(pltpu.make_async_copy(
            two_ref.at[:, part], two_hbm.at[0, :, part], store_sem.at[2 + pieces + piece]))
        stores[-1].start()
    for copy in stores:
        copy.wait()


def per_device(
    vectors, basis, potential, hop_table, soc_table, nbr_block, nbr_type, nbr_count, flip_block
):
    blocks, slots = nbr_block.shape
    types, width, _ = hop_table.shape
    vecs, kept = vectors.shape[1], basis.shape[1]
    dom_total = lax.axis_size("dom")
    group_doms = 4 if dom_total % 4 == 0 else 1
    groups = dom_total // group_doms
    reach = blocks + 2 * RANGE
    norm = float(2 * blocks * width * dom_total)
    cfg = (dom_total, group_doms, blocks, width, types, slots, vecs, kept, norm)
    count = blocks * width
    rows = blocks * vecs
    span_one, span_two = kept + vecs, kept + 2 * vecs
    vmem = pl.BlockSpec(memory_space=pltpu.VMEM)
    hbm = pl.BlockSpec(memory_space=pltpu.HBM)
    f32, bf16, i32 = jnp.float32, jnp.bfloat16, jnp.int32
    dma = pltpu.SemaphoreType.DMA
    shape = jax.ShapeDtypeStruct
    limit = 64 * 1000 * 1000
    one, image, small = pl.pallas_call(
        functools.partial(kernel, cfg),
        name="krylov",
        out_shape=(
            shape((vecs, count), f32),
            shape((vecs, count), f32),
            shape((3 * vecs, width), f32),
        ),
        in_specs=[hbm] * 9,
        out_specs=(hbm, hbm, vmem),
        scratch_shapes=[
            pltpu.VMEM((span_two + vecs, count), f32),
            pltpu.VMEM((span_two + vecs, vecs, width), f32),
            pltpu.VMEM((1, count), f32),
            pltpu.VMEM((types * width, width), bf16),
            pltpu.VMEM(soc_table.shape, bf16),
            pltpu.VMEM((slots, blocks), i32),
            pltpu.VMEM((slots, blocks), i32),
            pltpu.VMEM((1, blocks), i32),
            pltpu.VMEM((1, blocks), i32),
            pltpu.VMEM((blocks, width), i32),
            pltpu.SMEM((blocks, width), i32),
            pltpu.VMEM((2, rows, width), bf16),
            pltpu.VMEM((2, rows, width), bf16),
            pltpu.VMEM((2, 2 * RANGE * vecs, width), bf16),
            pltpu.VMEM((reach * types + 1 + blocks, vecs, width), f32),
            pltpu.VMEM((2, 2 * group_doms, vecs, width), f32),
            pltpu.VMEM((2, groups, vecs, width), f32),
            dma((12,)),
            dma((2, 3)), dma((2, 3)),
            dma((2, 2 * group_doms)), dma((2, 2 * group_doms)),
            dma((2, groups)), dma((2, groups)),
        ],
        compiler_params=pltpu.CompilerParams(
            collective_id=0, has_side_effects=True, vmem_limit_bytes=limit),
    )(
        vectors, basis, potential, hop_table.reshape(types * width, width), soc_table,
        nbr_block.T, nbr_type.T, nbr_count.reshape(1, blocks), flip_block.reshape(1, blocks))
    one, two, coef_one, coef_two = pl.pallas_call(
        functools.partial(finish, cfg),
        name="finish",
        out_shape=(
            shape((1, vecs, count), f32),
            shape((1, vecs, count), f32),
            shape((vecs, span_one + vecs), f32),
            shape((vecs, span_two + vecs), f32),
        ),
        in_specs=[vmem] + [hbm] * 4,
        out_specs=(hbm,) * 4,
        scratch_shapes=[
            pltpu.VMEM((span_two + vecs, count), f32),
            pltpu.VMEM((span_two + vecs, vecs, width), f32),
            pltpu.VMEM((vecs, count), f32),
            pltpu.VMEM((vecs, span_one + vecs), f32),
            pltpu.VMEM((vecs, span_two + vecs), f32),
            dma((4, 4)), dma((10,)),
        ],
        compiler_params=pltpu.CompilerParams(vmem_limit_bytes=limit),
    )(small, vectors, basis, one, image)
    return one, two, coef_one.T, coef_two.T


def solution(mesh):
    return jax.shard_map(
        per_device,
        mesh=mesh,
        in_specs=(
            P("spin", None, "dom"),
            P("spin", None, "dom"),
            P("spin", "dom"),
            P(),
            P(),
            P("dom", None),
            P("dom", None),
            P("dom"),
            P("dom"),
        ),
        out_specs=(P("spin", None, "dom"), P("spin", None, "dom"), P(), P()),
        check_vma=False,
    )
```

profile of v0, /device:TPU:0, one launch (start us, length us, event | category | flops | bytes accessed | tf_op | source)
XLA Modules:
  0.0 50.6 jit_solution(8675415930085793701)
XLA Ops:
  0.6 44.9 %krylov.1 = (f32[8,16384]{1,0:T(8,128)}, f32[8,16384]{1,0:T(8,128)}, f32[24,128]{1,0:T(8,128)}) custom-call(f32[1,8,16384]{2,1,0:T(8,128)} %vec_hbm.3, f32[1,16,16384]{2,1,0:T(8,128)} %basis_hbm.3, f32[1,16384]{1,0:T(1,128)} %pot_hbm.1, bf16[1024,128]{1,0:T(8,128)(2,1)} %bitcast.7, bf16[2,128,128]{2,1,0:T(8,128)(2,1)} %soc_hbm.1, s32[16,128]{1,0:T(8,128)} %bitcast.8, ...), custom_call_target="tpu_custom_call" | custom-call | tf_op jit(solution)/shard_map/krylov/pallas_call | solution.py:400
  45.6 5.0 %finish.1 = (f32[1,8,16384]{2,1,0:T(8,128)}, f32[1,8,16384]{2,1,0:T(8,128)}, f32[8,32]{1,0:T(8,128)}, f32[8,40]{1,0:T(8,128)}) custom-call(f32[24,128]{1,0:T(8,128)} %get-tuple-element.11.small_ref, f32[1,8,16384]{2,1,0:T(8,128)} %vec_hbm.3, f32[1,16,16384]{2,1,0:T(8,128)} %basis_hbm.3, f32[8,16384]{1,0:T(8,128)} %get-tuple-element.12.one_in_hbm, ...), custom_call_target="tpu_custom_call" | custom-call | tf_op jit(solution)/shard_map/finish/pallas_call | solution.py:438
where the time goes:
time: 50.8 us; the launch traced here: 50.6 us
  Pallas kernels  49.9 us (98%)
  between operations  0.64 us (1%)
    pallas_call x1, Pallas kernels, per_device(): pl.pallas_call(functools.partial(kernel, cfg), name='krylov', out_shape=(...  44.9 us
    pallas_call x1, Pallas kernels, per_device(): pl.pallas_call(functools.partial(finish, cfg), name='finish', out_shape=(...  4.99 us

commit v1 on v0

v1 whole, which is shorter than its diff:
```python
import functools
import jax
import jax.numpy as jnp
from jax import lax
from jax.experimental import pallas as pl
from jax.experimental.pallas import tpu as pltpu
from jax.sharding import PartitionSpec as P

RANGE = 8
STRIDE = 32
CHUNK = 16
MESH = pl.DeviceIdType.MESH
NT = (((1,), (1,)), ((), ()))
NN = (((1,), (0,)), ((), ()))
F32, BF16, I32 = jnp.float32, jnp.bfloat16, jnp.int32


def high_dot(left, right, dims):
    return lax.dot_general(
        left, right, dims, precision=lax.Precision.HIGHEST, preferred_element_type=F32
    )


def dot(left, right, dims):
    return lax.dot_general(left, right, dims, preferred_element_type=F32)


def split(value):
    low = value - value.astype(BF16).astype(F32)
    return jnp.concatenate([value, low], axis=0).astype(BF16)


def halves(value):
    high = value.astype(BF16)
    return high, (value - high.astype(F32)).astype(BF16)


def kernel(
    cfg,
    vec_hbm, basis_hbm, pot_hbm, hop_hbm, soc_hbm, nbr_hbm, type_hbm, count_hbm, flip_hbm,
    one_ref, split_ref, small_ref,
    vec_ref, basis_ref, pot_ref, hop_ref, soc_ref, nbr_ref, type_ref, count_ref, fliploc_ref,
    block_ref, edge_ref, major_ref, other_ref, near_ref, far_ref, prod_ref, edge_prod_ref,
    select_ref, edge_select_ref, fold_ref, stage_a_ref, stage_b_ref,
    load_sem, flip_send, flip_recv, edge_send, edge_recv, a_send, a_recv, b_send, b_recv,
):
    dom_total, group_doms, blocks, width, types, slots, vecs, kept, norm = cfg
    pair = 2 * vecs
    kept_groups = kept // vecs
    span_one = kept + vecs
    span_two = span_one + vecs
    rows_one = 2 * span_one
    rows_two = 2 * span_two
    count = blocks * width
    edge = RANGE * width
    kinds = (types + 1) * blocks

    sources = [
        (vec_hbm.at[0], vec_ref), (nbr_hbm, nbr_ref), (type_hbm, type_ref),
        (count_hbm, count_ref), (flip_hbm, fliploc_ref), (basis_hbm.at[0], basis_ref),
        (hop_hbm, hop_ref), (soc_hbm, soc_ref), (pot_hbm, pot_ref)]
    loads = [
        pltpu.make_async_copy(src, dst, load_sem.at[n]) for n, (src, dst) in enumerate(sources)]
    for copy in loads:
        copy.start()
    groups = dom_total // group_doms
    group_size = 2 * group_doms
    dom, spin = lax.axis_index("dom"), lax.axis_index("spin")
    rank_a = (dom % group_doms) * 2 + spin
    rank_b = dom // group_doms
    dom_base = rank_b * group_doms
    left, right = (dom + dom_total - 1) % dom_total, (dom + 1) % dom_total

    def peer_a(shift):
        other = (rank_a + shift) % group_size
        return (dom_base + other // 2, other % 2)

    def peer_b(shift):
        return (((rank_b + shift) % groups) * group_doms + dom % group_doms, spin)

    barrier = pltpu.get_barrier_semaphore()
    for shift in range(1, group_size):
        pl.semaphore_signal(barrier, inc=1, device_id=peer_a(shift), device_id_type=MESH)
    for shift in range(1, groups):
        pl.semaphore_signal(barrier, inc=1, device_id=peer_b(shift), device_id_type=MESH)
    for side in (left, right):
        pl.semaphore_signal(barrier, inc=1, device_id=(side, spin), device_id_type=MESH)

    lane = lax.broadcasted_iota(I32, (vecs, width), 1)
    row = lax.broadcasted_iota(I32, (vecs, width), 0)

    def cols(tile, size=1):
        return pl.ds(pl.multiple_of(tile * width, width), size * width)

    def flip_copy(app):
        return pltpu.make_async_remote_copy(
            src_ref=major_ref.at[app], dst_ref=other_ref.at[app],
            send_sem=flip_send.at[app], recv_sem=flip_recv.at[app],
            device_id=(dom, 1 - spin), device_id_type=MESH)

    def edge_copies(n, first, rows):
        part = pl.ds(first, rows)
        tail = pltpu.make_async_remote_copy(
            src_ref=split_ref.at[part, pl.ds(count - edge, edge)],
            dst_ref=edge_ref.at[part, pl.ds(0, edge)],
            send_sem=edge_send.at[n, 0], recv_sem=edge_recv.at[n, 0],
            device_id=(right, spin), device_id_type=MESH)
        head = pltpu.make_async_remote_copy(
            src_ref=split_ref.at[part, pl.ds(0, edge)],
            dst_ref=edge_ref.at[part, pl.ds(edge, edge)],
            send_sem=edge_send.at[n, 1], recv_sem=edge_recv.at[n, 1],
            device_id=(left, spin), device_id_type=MESH)
        return tail, head

    def to_major(value, scratch, base, store):
        for b in range(CHUNK):
            scratch[pl.ds(base + b * vecs, vecs), :] = value[:, b * width:(b + 1) * width]
        for k in range(vecs):
            store(k, scratch[pl.ds(base + k, CHUNK, stride=vecs), :].astype(BF16))

    def share(app, value):
        def stage(ref, send, recv, rank, size, peer, mine):
            ref[app, rank] = mine
            def copy(shift, slot):
                return pltpu.make_async_remote_copy(
                    src_ref=ref.at[app, rank], dst_ref=ref.at[app, slot],
                    send_sem=send.at[app, shift], recv_sem=recv.at[app, slot],
                    device_id=peer(shift), device_id_type=MESH)
            for shift in range(1, size):
                copy(shift, rank).start()
            for shift in range(1, size):
                copy(shift, (rank + size - shift) % size).wait_recv()
            for shift in range(1, size):
                copy(shift, rank).wait_send()
            total = ref[app, 0]
            for slot in range(1, size):
                total = total + ref[app, slot]
            return total
        value = stage(stage_a_ref, a_send, a_recv, rank_a, group_size, peer_a, value)
        if groups > 1:
            value = stage(stage_b_ref, b_send, b_recv, rank_b, groups, peer_b, value)
        return value * (1.0 / norm)

    def lanes(value, start, size):
        moved = value if start == 0 else pltpu.roll(value, width - start, 1)
        return jnp.where(lane < size, moved, 0.0)

    def tall(pieces):
        pad = width - vecs * len(pieces)
        return jnp.concatenate(list(pieces) + [jnp.zeros((pad, width), F32)], axis=0)

    def folded(value):
        wide = value.shape[1]
        fold_ref[:, pl.ds(0, wide)] = value[:vecs] + value[vecs:]
        both = fold_ref[...]
        both = both + pltpu.roll(both, width - vecs, 1)
        out = jnp.where(lane < vecs, both, 0.0)
        for g in range(1, wide // pair):
            inside = (lane >= vecs * g) & (lane < vecs * (g + 1))
            out = jnp.where(inside, pltpu.roll(both, width - vecs * g, 1), out)
        return out

    def gram(first, rows, size, start, stop):
        part = pl.ds(start * width, (stop - start) * width)
        return dot(split_ref[pl.ds(first, rows), part], split_ref[pl.ds(0, size), part], NT)

    def factor(first_t, image_gram, span_gram, span_count):
        total_t = 2.0 * first_t - high_dot(first_t, span_gram, NT)
        moved = high_dot(total_t, span_gram, NT) - first_t
        square = image_gram + high_dot(moved, tall([total_t]), NT) - high_dot(
            total_t, tall([first_t]), NT)
        table = jnp.where(lane < vecs, square, jnp.where(lane == row + vecs, 1.0, 0.0))
        table = table - pltpu.roll(total_t, pair, 1)
        lower = jnp.zeros((vecs, width), F32)
        for j in range(vecs):
            column = jnp.broadcast_to(table[:, j:j + 1], (vecs, width))
            pivot_row = jnp.broadcast_to(table[j:j + 1, :], (vecs, width))
            pivot = jnp.broadcast_to(column[j:j + 1, :], (vecs, width))
            scale = 1.0 / jnp.sqrt(pivot)
            lower = jnp.where((lane == j) & (row >= j), column * scale, lower)
            pivot_row = pivot_row * scale
            table = jnp.where(
                row == j, pivot_row, jnp.where(row > j, table - column * scale * pivot_row, table))
        mixer = jnp.zeros((vecs, width), F32)
        for g in range(span_count // vecs + 1):
            source = pair + vecs * g if g < span_count // vecs else vecs
            moved = pltpu.roll(table, (pair * g - source) % width, 1)
            mixer = jnp.where((lane >= pair * g) & (lane < pair * g + vecs), moved, mixer)
        mixer = mixer + pltpu.roll(mixer, vecs, 1)
        low = mixer - mixer.astype(BF16).astype(F32)
        return total_t + pltpu.roll(lower, span_count, 1), jnp.concatenate([mixer, low], axis=0)

    def products(app):
        source = major_ref[app].reshape(vecs * blocks, width)

        def body(two, carry):
            weights = hop_ref[pl.ds(pl.multiple_of(two * 2 * width, 2 * width), 2 * width), :]
            out = dot(source, weights, NT)
            for half in range(2):
                at = pl.multiple_of((two * 2 + half) * blocks, blocks)
                for k in range(vecs):
                    high, low = halves(
                        out[k * blocks:(k + 1) * blocks, half * width:(half + 1) * width])
                    side = pl.ds((k % 2) * width, width)
                    prod_ref[k // 2, pl.ds(at, blocks), side] = high
                    prod_ref[k // 2, pl.ds(kinds + at, blocks), side] = low
            return carry
        lax.fori_loop(0, types // 2, body, 0)

    def flip_products(app):
        out = dot(other_ref[app].reshape(vecs * blocks, width), soc_ref[spin], NT)
        for k in range(vecs):
            high, low = halves(out[k * blocks:(k + 1) * blocks])
            side = pl.ds((k % 2) * width, width)
            prod_ref[k // 2, pl.ds(types * blocks, blocks), side] = high
            prod_ref[k // 2, pl.ds(kinds + types * blocks, blocks), side] = low

    def gather():
        def body(two, carry):
            out = dot(select_ref[...], prod_ref[two], NN)
            for half in range(2):
                for i in range(blocks // vecs):
                    block_ref[pl.ds(i * vecs * vecs + 2 * two + half, vecs, stride=vecs), :] = (
                        out[i * vecs:(i + 1) * vecs, half * width:(half + 1) * width])
            return carry
        lax.fori_loop(0, vecs // 2, body, 0)

    def edge_gather():
        reach = 2 * RANGE
        source = far_ref[...].reshape(vecs * reach, width)

        def body(two, carry):
            weights = hop_ref[pl.ds(pl.multiple_of(two * 2 * width, 2 * width), 2 * width), :]
            out = dot(source, weights, NT)
            for half in range(2):
                at = pl.multiple_of((two * 2 + half) * reach, reach)
                for k in range(vecs):
                    high, low = halves(
                        out[k * reach:(k + 1) * reach, half * width:(half + 1) * width])
                    side = pl.ds((k % 2) * width, width)
                    edge_prod_ref[k // 2, pl.ds(at, reach), side] = high
                    edge_prod_ref[k // 2, pl.ds(types * reach + at, reach), side] = low
            return carry
        lax.fori_loop(0, types // 2, body, 0, unroll=True)
        for two in range(vecs // 2):
            out = dot(edge_select_ref[...], edge_prod_ref[two], NN)
            for half in range(2):
                for end, base in enumerate((0, (blocks - RANGE) * vecs)):
                    at = pl.ds(base + 2 * two + half, RANGE, stride=vecs)
                    block_ref[at, :] = block_ref[at, :] + out[
                        end * RANGE:(end + 1) * RANGE, half * width:(half + 1) * width]

    def assemble(field_ref, first, low, high):
        def body(block, carry):
            image = pot_ref[pl.ds(0, 1), cols(block)] * field_ref[:, cols(block)]
            at = pl.multiple_of(block * vecs, vecs)
            image = image + block_ref[pl.ds(at, vecs), :]
            split_ref[pl.ds(first, pair), cols(block)] = split(image)
            return carry
        lax.fori_loop(low, high, body, 0, unroll=8)

    def round_body(chunk, carry):
        value = vec_ref[:, cols(chunk * CHUNK, CHUNK)]
        split_ref[pl.ds(2 * kept, pair), cols(chunk * CHUNK, CHUNK)] = split(value)

        def store(k, rounded):
            major_ref[0, k, pl.ds(pl.multiple_of(chunk * CHUNK, CHUNK), CHUNK), :] = rounded
        to_major(value, block_ref, chunk * CHUNK * vecs, store)
        return carry

    def store_far(k, rounded):
        far_ref[k] = rounded

    chunks = blocks // CHUNK
    loads[0].wait()
    round_body(0, 0)
    round_body(chunks - 1, 0)
    pl.semaphore_wait(barrier, group_size - 1 + groups - 1 + 2)
    vec_edges = edge_copies(0, 2 * kept, pair)
    for copy in vec_edges:
        copy.start()
    lax.fori_loop(1, chunks - 1, round_body, 0)
    flip_one = flip_copy(0)
    flip_one.start()
    for copy in loads[1:6]:
        copy.wait()

    def split_basis(chunk, carry):
        part = cols(chunk * 4, 4)
        for g in range(kept_groups):
            split_ref[pl.ds(g * pair, pair), part] = split(basis_ref[pl.ds(g * vecs, vecs), part])
        return carry
    lax.fori_loop(0, blocks // 4, split_basis, 0, unroll=2)
    basis_edges = edge_copies(1, 0, 2 * kept)
    for copy in basis_edges:
        copy.start()

    local = lax.broadcasted_iota(I32, (slots, blocks), 1)
    slot_at = lax.broadcasted_iota(I32, (slots, blocks), 0)
    shift = nbr_ref[...] - (dom * blocks + local) + RANGE
    total = dom_total * blocks
    shift = jnp.where(shift < 0, shift + total, shift)
    shift = jnp.where(shift >= total, shift - total, shift)
    place = local + shift - RANGE
    live = slot_at < count_ref[...]
    inside = (place >= 0) & (place < blocks)
    code = jnp.where(live & inside, type_ref[...] * STRIDE + shift, -1)
    edge_code = jnp.where(place < 0, place + RANGE, place - blocks + RANGE)
    edge_code = jnp.where(live & ~inside, type_ref[...] * (2 * RANGE) + edge_code, -1)

    def counts(codes, base):
        wanted = row + base
        parts = [jnp.where(codes[s:s + 1, :] == wanted, 1.0, 0.0) for s in range(slots)]
        while len(parts) > 1:
            parts = [parts[p] + parts[p + 1] for p in range(0, len(parts), 2)]
        return parts[0]

    wide_row = lax.broadcasted_iota(I32, (width, width), 0)
    wide_lane = lax.broadcasted_iota(I32, (width, width), 1)
    band = (wide_lane - wide_row <= RANGE) & (wide_row - wide_lane <= RANGE)
    per_tile = width // STRIDE
    blank = jnp.zeros((vecs, width), F32)
    for tile in range(types // per_tile):
        pieces = []
        for r in range(width // vecs):
            live_rows = (r * vecs) % STRIDE <= 2 * RANGE
            pieces.append(counts(code, tile * width + r * vecs) if live_rows else blank)
        table = jnp.concatenate(pieces, axis=0).T
        for t in range(per_tile):
            moved = pltpu.roll(
                table, (-RANGE - STRIDE * t) % width, 1, stride=1, stride_axis=0)
            picked = jnp.where(band, moved, 0.0).astype(BF16)
            at = (tile * per_tile + t) * blocks
            select_ref[:, pl.ds(at, blocks)] = picked
            select_ref[:, pl.ds(kinds + at, blocks)] = picked
    flip_local = fliploc_ref[...] - dom * blocks
    picked = jnp.where(flip_local == wide_row, 1.0, 0.0).T.astype(BF16)
    select_ref[:, pl.ds(types * blocks, blocks)] = picked
    select_ref[:, pl.ds(kinds + types * blocks, blocks)] = picked
    table = jnp.concatenate(
        [counts(edge_code, r * vecs) for r in range(width // vecs)], axis=0).T
    picked = jnp.concatenate([table[:RANGE], table[blocks - RANGE:]], axis=0).astype(BF16)
    edge_select_ref[:, pl.ds(0, width)] = picked
    edge_select_ref[:, pl.ds(width, width)] = picked

    fold_ref[...] = jnp.zeros((vecs, width), F32)
    low_gram = gram(0, rows_one, rows_one, 0, blocks)
    packed_low = jnp.zeros((vecs, width), F32)
    for g in range(span_one // vecs):
        piece = folded(low_gram[g * pair:(g + 1) * pair])
        packed_low = packed_low + pltpu.roll(piece, span_two + g * span_one, 1)
    for copy in loads[6:]:
        copy.wait()

    products(0)
    flip_one.wait_recv()
    flip_products(0)
    gather()
    assemble(vec_ref, rows_one, RANGE, blocks - RANGE)
    result = gram(rows_one, pair, rows_two, RANGE, blocks - RANGE)
    for copy in vec_edges:
        copy.wait_recv()
    value = edge_ref[pl.ds(2 * kept, pair), :].astype(F32)[:vecs]
    to_major(value, near_ref, 0, store_far)
    edge_gather()
    assemble(vec_ref, rows_one, 0, RANGE)
    assemble(vec_ref, rows_one, blocks - RANGE, blocks)
    image_edges = edge_copies(2, rows_one, pair)
    for copy in image_edges:
        copy.start()
    result = result + gram(rows_one, pair, rows_two, 0, RANGE)
    result = result + gram(rows_one, pair, rows_two, blocks - RANGE, blocks)
    packed = share(0, folded(result) + packed_low)
    span_gram = tall(
        [lanes(packed, span_two + g * span_one, span_one) for g in range(span_one // vecs)])
    coefs, mixer = factor(
        lanes(packed, 0, span_one), lanes(packed, span_one, vecs), span_gram, span_one)
    small_ref[pl.ds(0, vecs), :] = coefs
    mixer = mixer.astype(BF16)[:, :rows_two]
    for copy in image_edges:
        copy.wait_send()
    for copy in image_edges + basis_edges:
        copy.wait_recv()

    def mix_body(chunk, carry):
        part = cols(chunk * CHUNK, CHUNK)
        out = dot(mixer, split_ref[pl.ds(0, rows_two), part], NN)
        value = out[:vecs] + out[vecs:]
        one_ref[:, part] = value
        split_ref[pl.ds(rows_one, pair), part] = split(value)

        def store(k, rounded):
            major_ref[1, k, pl.ds(pl.multiple_of(chunk * CHUNK, CHUNK), CHUNK), :] = rounded
        to_major(value, block_ref, chunk * CHUNK * vecs, store)
        return carry
    lax.fori_loop(0, chunks, mix_body, 0)
    flip_two = flip_copy(1)
    flip_two.start()
    products(1)
    out = dot(mixer, edge_ref[...], NN)
    to_major(out[:vecs] + out[vecs:], near_ref, 0, store_far)
    early = folded(gram(rows_one, pair, rows_two, 0, blocks))
    flip_two.wait_recv()
    flip_products(1)
    gather()
    edge_gather()
    assemble(one_ref, rows_two, 0, blocks)
    result = folded(gram(rows_two, pair, rows_two + pair, 0, blocks))
    packed = share(1, result + pltpu.roll(early, 64, 1))
    low = jnp.concatenate(
        [jnp.zeros((span_one, width), F32), lanes(packed, 64, span_two),
         jnp.zeros((width - span_two, width), F32)], axis=0)
    span_gram = span_gram + low + jnp.where(
        (wide_row < span_one) & (wide_lane >= span_one), low.T, 0.0)
    coefs, mixer = factor(
        lanes(packed, 0, span_two), lanes(packed, span_two, vecs), span_gram, span_two)
    small_ref[pl.ds(vecs, vecs), :] = coefs
    small_ref[pl.ds(pair, pair), :] = mixer
    for copy in vec_edges + basis_edges:
        copy.wait_send()
    flip_one.wait_send()
    flip_two.wait_send()


def finish(
    cfg, small_ref, split_ref, one_ref,
    one_hbm, two_hbm, coef_one_hbm, coef_two_hbm,
    two_ref, cut_one_ref, cut_two_ref, store_sem,
):
    _, _, blocks, width, _, _, vecs, kept, _ = cfg
    span_one = kept + vecs
    span_two = span_one + vecs
    pieces = 8
    size = blocks // pieces * width
    stores = [pltpu.make_async_copy(one_ref, one_hbm.at[0], store_sem.at[0])]
    stores[-1].start()
    mixer = small_ref[pl.ds(2 * vecs, 2 * vecs), :].astype(BF16)[:, :2 * (span_two + vecs)]
    for piece in range(pieces):
        part = pl.ds(piece * size, size)
        out = dot(mixer, split_ref[:, part], NN)
        two_ref[:, part] = out[:vecs] + out[vecs:]
        stores.append(pltpu.make_async_copy(
            two_ref.at[:, part], two_hbm.at[0, :, part], store_sem.at[1 + piece]))
        stores[-1].start()
    cut_one_ref[...] = small_ref[pl.ds(0, vecs), :span_one + vecs]
    cut_two_ref[...] = small_ref[pl.ds(vecs, vecs), :span_two + vecs]
    stores.append(pltpu.make_async_copy(cut_one_ref, coef_one_hbm, store_sem.at[1 + pieces]))
    stores.append(pltpu.make_async_copy(cut_two_ref, coef_two_hbm, store_sem.at[2 + pieces]))
    for copy in stores[-2:]:
        copy.start()
    for copy in stores:
        copy.wait()


def per_device(
    vectors, basis, potential, hop_table, soc_table, nbr_block, nbr_type, nbr_count, flip_block
):
    blocks, slots = nbr_block.shape
    types, width, _ = hop_table.shape
    vecs, kept = vectors.shape[1], basis.shape[1]
    dom_total = lax.axis_size("dom")
    group_doms = 4 if dom_total % 4 == 0 else 1
    groups = dom_total // group_doms
    norm = float(2 * blocks * width * dom_total)
    cfg = (dom_total, group_doms, blocks, width, types, slots, vecs, kept, norm)
    count = blocks * width
    pair = 2 * vecs
    span_one, span_two = kept + vecs, kept + 2 * vecs
    kinds = (types + 1) * blocks
    vmem = pl.BlockSpec(memory_space=pltpu.VMEM)
    hbm = pl.BlockSpec(memory_space=pltpu.HBM)
    dma = pltpu.SemaphoreType.DMA
    shape = jax.ShapeDtypeStruct
    one, parts, small = pl.pallas_call(
        functools.partial(kernel, cfg),
        name="krylov",
        out_shape=(
            pltpu.VMEM((vecs, count), F32),
            pltpu.VMEM((2 * (span_two + vecs), count), BF16),
            pltpu.VMEM((4 * vecs, width), F32),
        ),
        in_specs=[hbm] * 9,
        out_specs=(vmem, vmem, vmem),
        scratch_shapes=[
            pltpu.VMEM((vecs, count), F32),
            pltpu.VMEM((kept, count), F32),
            pltpu.VMEM((1, count), F32),
            pltpu.VMEM((types * width, width), BF16),
            pltpu.VMEM(soc_table.shape, BF16),
            pltpu.VMEM((slots, blocks), I32),
            pltpu.VMEM((slots, blocks), I32),
            pltpu.VMEM((1, blocks), I32),
            pltpu.VMEM((1, blocks), I32),
            pltpu.VMEM((blocks * vecs, width), F32),
            pltpu.VMEM((2 * span_two, 2 * RANGE * width), BF16),
            pltpu.VMEM((2, vecs, blocks, width), BF16),
            pltpu.VMEM((2, vecs, blocks, width), BF16),
            pltpu.VMEM((2 * RANGE * vecs, width), F32),
            pltpu.VMEM((vecs, 2 * RANGE, width), BF16),
            pltpu.VMEM((vecs // 2, 2 * kinds, 2 * width), BF16),
            pltpu.VMEM((vecs // 2, 4 * RANGE * types, 2 * width), BF16),
            pltpu.VMEM((blocks, 2 * kinds), BF16),
            pltpu.VMEM((2 * RANGE, 4 * RANGE * types), BF16),
            pltpu.VMEM((vecs, width), F32),
            pltpu.VMEM((2, 2 * group_doms, vecs, width), F32),
            pltpu.VMEM((2, groups, vecs, width), F32),
            dma((9,)),
            dma((2,)), dma((2,)),
            dma((3, 2)), dma((3, 2)),
            dma((2, 2 * group_doms)), dma((2, 2 * group_doms)),
            dma((2, groups)), dma((2, groups)),
        ],
        compiler_params=pltpu.CompilerParams(
            collective_id=0, has_side_effects=True, vmem_limit_bytes=32 * 1024 * 1024),
    )(
        vectors, basis, potential, hop_table.reshape(types * width, width), soc_table,
        nbr_block.T, nbr_type.T, nbr_count.reshape(1, blocks), flip_block.reshape(1, blocks))
    one, two, coef_one, coef_two = pl.pallas_call(
        functools.partial(finish, cfg),
        name="finish",
        out_shape=(
            shape((1, vecs, count), F32),
            shape((1, vecs, count), F32),
            shape((vecs, span_one + vecs), F32),
            shape((vecs, span_two + vecs), F32),
        ),
        in_specs=[vmem, vmem, vmem],
        out_specs=(hbm,) * 4,
        scratch_shapes=[
            pltpu.VMEM((vecs, count), F32),
            pltpu.VMEM((vecs, span_one + vecs), F32),
            pltpu.VMEM((vecs, span_two + vecs), F32),
            dma((11,)),
        ],
        compiler_params=pltpu.CompilerParams(vmem_limit_bytes=16 * 1024 * 1024),
    )(small, parts, one)
    return one, two, coef_one.T, coef_two.T


def solution(mesh):
    return jax.shard_map(
        per_device,
        mesh=mesh,
        in_specs=(
            P("spin", None, "dom"),
            P("spin", None, "dom"),
            P("spin", "dom"),
            P(),
            P(),
            P("dom", None),
            P("dom", None),
            P("dom"),
            P("dom"),
        ),
        out_specs=(P("spin", None, "dom"), P("spin", None, "dom"), P(), P()),
        check_vma=False,
    )
```

time: 50.8 us -> 48.4 us (0.953)
  Pallas kernels: 49.9 us -> 39.7 us
  local copies, waits for them, and re-layouts: 0 us -> 7.59 us
    unnamed x0 -> x18, local copies, waits for them, and re-layouts: none -> 7.59 us
    pallas_call x1, Pallas kernels: 44.9 us -> 38.5 us  [per_device(): pl.pallas_call(functools.partial(kernel, cfg), name='krylov', out_shape=(...]
    pallas_call x1, Pallas kernels: 4.99 us -> 1.2 us  [per_device(): pl.pallas_call(functools.partial(finish, cfg), name='finish', out_shape=(...]
where the time goes in v1:
time: 48.4 us; the launch traced here: 48 us
  Pallas kernels  39.7 us (82%)
  local copies, waits for them, and re-layouts  7.59 us (16%)
  between operations  0.66 us (1%)
    pallas_call x1, Pallas kernels, per_device(): pl.pallas_call(functools.partial(kernel, cfg), name='krylov', out_shape=(...  38.5 us
    unnamed x18, local copies, waits for them, and re-layouts  7.59 us
    pallas_call x1, Pallas kernels, per_device(): pl.pallas_call(functools.partial(finish, cfg), name='finish', out_shape=(...  1.2 us

profile of v1, /device:TPU:0, one launch (start us, length us, event | category | flops | bytes accessed | tf_op | source)
XLA Modules:
  0.0 48.0 jit_solution(5373085779071817506)
XLA Ops:
  0.6 0.0 copy-start
  0.6 1.2 %copy-done = f32[1,16,16384]{2,1,0:T(8,128)S(1)} copy-done((f32[1,16,16384]{2,1,0:T(8,128)S(1)}, f32[1,16,16384]{2,1,0:T(8,128)}, u32[]{:S(2)}) %copy-start) | copy-done | bytes 1048600
  1.9 0.0 copy-start.1
  1.9 1.0 %copy-done.1 = f32[1,8,16384]{2,1,0:T(8,128)S(1)} copy-done((f32[1,8,16384]{2,1,0:T(8,128)S(1)}, f32[1,8,16384]{2,1,0:T(8,128)}, u32[]{:S(2)}) %copy-start.1) | copy-done | bytes 524312
  2.9 0.0 copy-start.2
  2.9 0.9 %copy-done.2 = bf16[8,128,128]{2,1,0:T(8,128)(2,1)S(1)} copy-done((bf16[8,128,128]{2,1,0:T(8,128)(2,1)S(1)}, bf16[8,128,128]{2,1,0:T(8,128)(2,1)}, u32[]{:S(2)}) %copy-start.2) | copy-done | bytes 262168
  3.9 0.0 copy-start.3
  3.9 0.8 %copy-done.3 = f32[1,16384]{1,0:T(1,128)S(1)} copy-done((f32[1,16384]{1,0:T(1,128)S(1)}, f32[1,16384]{1,0:T(1,128)}, u32[]{:S(2)}) %copy-start.3) | copy-done | bytes 65560
  4.7 0.0 copy-start.4
  4.7 0.8 %copy-done.4 = bf16[2,128,128]{2,1,0:T(8,128)(2,1)S(1)} copy-done((bf16[2,128,128]{2,1,0:T(8,128)(2,1)S(1)}, bf16[2,128,128]{2,1,0:T(8,128)(2,1)}, u32[]{:S(2)}) %copy-start.4) | copy-done | bytes 65560
  5.5 0.0 copy-start.5
  5.5 0.7 %copy-done.5 = s32[128,16]{0,1:T(8,128)S(1)} copy-done((s32[128,16]{0,1:T(8,128)S(1)}, s32[128,16]{0,1:T(8,128)}, u32[]{:S(2)}) %copy-start.5) | copy-done | bytes 8216
  6.2 0.0 copy-start.6
  6.2 0.7 %copy-done.6 = s32[128,16]{0,1:T(8,128)S(1)} copy-done((s32[128,16]{0,1:T(8,128)S(1)}, s32[128,16]{0,1:T(8,128)}, u32[]{:S(2)}) %copy-start.6) | copy-done | bytes 8216
  6.9 0.0 copy-start.7
  6.9 0.7 %copy-done.7 = s32[128]{0:T(128)S(1)} copy-done((s32[128]{0:T(128)S(1)}, s32[128]{0:T(128)}, u32[]{:S(2)}) %copy-start.7) | copy-done | bytes 536
  7.6 0.0 copy-start.8
  7.6 0.7 %copy-done.8 = s32[128]{0:T(128)S(1)} copy-done((s32[128]{0:T(128)S(1)}, s32[128]{0:T(128)}, u32[]{:S(2)}) %copy-start.8) | copy-done | bytes 536
  8.2 38.5 %krylov.1 = (f32[8,16384]{1,0:T(8,128)S(1)}, bf16[80,16384]{1,0:T(8,128)(2,1)S(1)}, f32[32,128]{1,0:T(8,128)S(1)}) custom-call(f32[1,8,16384]{2,1,0:T(8,128)S(1)} %copy-done.1, f32[1,16,16384]{2,1,0:T(8,128)S(1)} %copy-done, f32[1,16384]{1,0:T(1,128)S(1)} %copy-done.3, bf16[1024,128]{1,0:T(8,128)(2,1)S(1)} %bitcast.7, bf16[2,128,128]{2,1,0:T(8,128)(2,1)S(1)} %copy-done.4, ...), custom_call_target="tpu_custom_call" | custom-call | tf_op jit(solution)/shard_map/krylov/pallas_call | solution.py:474
  46.8 1.2 %finish.1 = (f32[1,8,16384]{2,1,0:T(8,128)}, f32[1,8,16384]{2,1,0:T(8,128)}, f32[8,32]{1,0:T(8,128)}, f32[8,40]{1,0:T(8,128)}) custom-call(f32[32,128]{1,0:T(8,128)S(1)} %get-tuple-element.11.small_ref, bf16[80,16384]{1,0:T(8,128)(2,1)S(1)} %get-tuple-element.12.split_ref, f32[8,16384]{1,0:T(8,128)S(1)} %get-tuple-element.13.one_ref), custom_call_target="tpu_custom_call" | custom-call | tf_op jit(solution)/shard_map/finish/pallas_call | solution.py:518
Async XLA Ops:
  0.6 1.2 %copy-start = (f32[1,16,16384]{2,1,0:T(8,128)S(1)}, f32[1,16,16384]{2,1,0:T(8,128)}, u32[]{:S(2)}) copy-start(f32[1,16,16384]{2,1,0:T(8,128)} %basis_hbm.1) | copy-start | bytes 3145732
  1.9 1.0 %copy-start.1 = (f32[1,8,16384]{2,1,0:T(8,128)S(1)}, f32[1,8,16384]{2,1,0:T(8,128)}, u32[]{:S(2)}) copy-start(f32[1,8,16384]{2,1,0:T(8,128)} %vec_hbm.1) | copy-start | bytes 1572868
  2.9 0.9 %copy-start.2 = (bf16[8,128,128]{2,1,0:T(8,128)(2,1)S(1)}, bf16[8,128,128]{2,1,0:T(8,128)(2,1)}, u32[]{:S(2)}) copy-start(bf16[8,128,128]{2,1,0:T(8,128)(2,1)} %param.12) | copy-start | bytes 786436
  3.9 0.8 %copy-start.3 = (f32[1,16384]{1,0:T(1,128)S(1)}, f32[1,16384]{1,0:T(1,128)}, u32[]{:S(2)}) copy-start(f32[1,16384]{1,0:T(1,128)} %pot_hbm.1) | copy-start | bytes 196612
  4.7 0.8 %copy-start.4 = (bf16[2,128,128]{2,1,0:T(8,128)(2,1)S(1)}, bf16[2,128,128]{2,1,0:T(8,128)(2,1)}, u32[]{:S(2)}) copy-start(bf16[2,128,128]{2,1,0:T(8,128)(2,1)} %soc_hbm.1) | copy-start | bytes 196612
  5.5 0.7 %copy-start.5 = (s32[128,16]{0,1:T(8,128)S(1)}, s32[128,16]{0,1:T(8,128)}, u32[]{:S(2)}) copy-start(s32[128,16]{0,1:T(8,128)} %param.14) | copy-start | bytes 24580
  6.2 0.7 %copy-start.6 = (s32[128,16]{0,1:T(8,128)S(1)}, s32[128,16]{0,1:T(8,128)}, u32[]{:S(2)}) copy-start(s32[128,16]{0,1:T(8,128)} %param.15) | copy-start | bytes 24580
  6.9 0.7 %copy-start.7 = (s32[128]{0:T(128)S(1)}, s32[128]{0:T(128)}, u32[]{:S(2)}) copy-start(s32[128]{0:T(128)} %param.16) | copy-start | bytes 1540
  7.6 0.7 %copy-start.8 = (s32[128]{0:T(128)S(1)}, s32[128]{0:T(128)}, u32[]{:S(2)}) copy-start(s32[128]{0:T(128)} %param.17) | copy-start | bytes 1540

commit v2 on v1

--- a/solution.py
+++ b/solution.py
@@ -512,9 +512,9 @@
         ],
         compiler_params=pltpu.CompilerParams(
             collective_id=0, has_side_effects=True, vmem_limit_bytes=32 * 1024 * 1024),
-    )(
+    )(*[pltpu.with_memory_space_constraint(value, pltpu.HBM) for value in (
         vectors, basis, potential, hop_table.reshape(types * width, width), soc_table,
-        nbr_block.T, nbr_type.T, nbr_count.reshape(1, blocks), flip_block.reshape(1, blocks))
+        nbr_block.T, nbr_type.T, nbr_count.reshape(1, blocks), flip_block.reshape(1, blocks))])
     one, two, coef_one, coef_two = pl.pallas_call(
         functools.partial(finish, cfg),
         name="finish",

time: 48.4 us -> 40.2 us (0.83)
  local copies, waits for them, and re-layouts: 7.59 us -> 0 us
    unnamed x18 -> x0, local copies, waits for them, and re-layouts: 7.59 us -> none
where the time goes in v2:
time: 40.2 us; the launch traced here: 40.1 us
  Pallas kernels  39.4 us (98%)
  between operations  0.64 us (2%)
    pallas_call x1, Pallas kernels, per_device(): pl.pallas_call(functools.partial(kernel, cfg), name='krylov', out_shape=(...  38.2 us
    pallas_call x1, Pallas kernels, per_device(): pl.pallas_call(functools.partial(finish, cfg), name='finish', out_shape=(...  1.2 us

profile of v2, /device:TPU:0, one launch (start us, length us, event | category | flops | bytes accessed | tf_op | source)
XLA Modules:
  0.0 40.1 jit_solution(15851623138343086978)
XLA Ops:
  0.6 38.2 %krylov.1 = (f32[8,16384]{1,0:T(8,128)S(1)}, bf16[80,16384]{1,0:T(8,128)(2,1)S(1)}, f32[32,128]{1,0:T(8,128)S(1)}) custom-call(f32[1,8,16384]{2,1,0:T(8,128)} %vec_hbm.1, f32[1,16,16384]{2,1,0:T(8,128)} %basis_hbm.1, f32[1,16384]{1,0:T(1,128)} %pot_hbm.1, bf16[1024,128]{1,0:T(8,128)(2,1)} %bitcast.7, bf16[2,128,128]{2,1,0:T(8,128)(2,1)} %soc_hbm.1, ...), custom_call_target="tpu_custom_call" | custom-call | tf_op jit(solution)/shard_map/krylov/pallas_call | solution.py:474
  38.9 1.2 %finish.1 = (f32[1,8,16384]{2,1,0:T(8,128)}, f32[1,8,16384]{2,1,0:T(8,128)}, f32[8,32]{1,0:T(8,128)}, f32[8,40]{1,0:T(8,128)}) custom-call(f32[32,128]{1,0:T(8,128)S(1)} %get-tuple-element.11.small_ref, bf16[80,16384]{1,0:T(8,128)(2,1)S(1)} %get-tuple-element.12.split_ref, f32[8,16384]{1,0:T(8,128)S(1)} %get-tuple-element.13.one_ref), custom_call_target="tpu_custom_call" | custom-call | tf_op jit(solution)/shard_map/finish/pallas_call | solution.py:518

commit v3 on v2

v3 whole, which is shorter than its diff:
```python
import functools
import jax
import jax.numpy as jnp
from jax import lax
from jax.experimental import pallas as pl
from jax.experimental.pallas import tpu as pltpu
from jax.sharding import PartitionSpec as P

RANGE = 8
STRIDE = 32
CHUNK = 16
MESH = pl.DeviceIdType.MESH
NT = (((1,), (1,)), ((), ()))
NN = (((1,), (0,)), ((), ()))
F32, BF16, I32 = jnp.float32, jnp.bfloat16, jnp.int32


def high_dot(left, right, dims):
    return lax.dot_general(
        left, right, dims, precision=lax.Precision.HIGHEST, preferred_element_type=F32
    )


def dot(left, right, dims):
    return lax.dot_general(left, right, dims, preferred_element_type=F32)


def split(value):
    low = value - value.astype(BF16).astype(F32)
    return jnp.concatenate([value, low], axis=0).astype(BF16)


def halves(value):
    high = value.astype(BF16)
    return high, (value - high.astype(F32)).astype(BF16)


def kernel(
    cfg,
    vec_hbm, basis_hbm, pot_hbm, hop_hbm, soc_hbm, nbr_hbm, type_hbm, count_hbm, flip_hbm,
    one_ref, split_ref, small_ref,
    vec_ref, basis_ref, pot_ref, hop_ref, soc_ref, nbr_ref, type_ref, count_ref, fliploc_ref,
    block_ref, edge_ref, major_ref, other_ref, near_ref, far_ref, prod_ref, edge_prod_ref,
    select_ref, edge_select_ref, fold_ref, weight_ref, stage_a_ref, stage_b_ref,
    all_one_ref, all_two_ref,
    load_sem, flip_send, flip_recv, edge_send, edge_recv, a_send, a_recv, b_send, b_recv,
    all_send, all_recv,
):
    dom_total, group_doms, blocks, width, types, slots, vecs, kept, norm, direct = cfg
    pair = 2 * vecs
    kept_groups = kept // vecs
    span_one = kept + vecs
    span_two = span_one + vecs
    rows_one = 2 * span_one
    rows_two = 2 * span_two
    kinds = types + 1
    devices = 2 * dom_total

    sources = [
        (vec_hbm.at[0], vec_ref), (nbr_hbm, nbr_ref), (type_hbm, type_ref),
        (count_hbm, count_ref), (flip_hbm, fliploc_ref), (basis_hbm.at[0], basis_ref),
        (hop_hbm, hop_ref), (soc_hbm, soc_ref), (pot_hbm, pot_ref)]
    loads = [
        pltpu.make_async_copy(src, dst, load_sem.at[n]) for n, (src, dst) in enumerate(sources)]
    for copy in loads:
        copy.start()
    groups = dom_total // group_doms
    group_size = 2 * group_doms
    dom, spin = lax.axis_index("dom"), lax.axis_index("spin")
    rank_a = (dom % group_doms) * 2 + spin
    rank_b = dom // group_doms
    dom_base = rank_b * group_doms
    left, right = (dom + dom_total - 1) % dom_total, (dom + 1) % dom_total

    def peer_a(shift):
        other = (rank_a + shift) % group_size
        return (dom_base + other // 2, other % 2)

    def peer_b(shift):
        return (((rank_b + shift) % groups) * group_doms + dom % group_doms, spin)

    far_first = sorted(range(dom_total), key=lambda shift: -min(shift, dom_total - shift))

    def everyone():
        for shift in far_first:
            ahead = dom + shift
            target = jnp.where(ahead >= dom_total, ahead - dom_total, ahead)
            if shift:
                yield (target, spin)
            yield (target, 1 - spin)

    barrier = pltpu.get_barrier_semaphore()
    if direct:
        greeted = list(everyone())
    else:
        greeted = [peer_a(shift) for shift in range(1, group_size)]
        greeted += [peer_b(shift) for shift in range(1, groups)]
        greeted += [(left, spin), (right, spin)]
    for target in greeted:
        pl.semaphore_signal(barrier, inc=1, device_id=target, device_id_type=MESH)

    lane = lax.broadcasted_iota(I32, (vecs, width), 1)
    row = lax.broadcasted_iota(I32, (vecs, width), 0)

    def cols(tile, size=1):
        return pl.ds(pl.multiple_of(tile * width, width), size * width)

    def flip_copy(app):
        return pltpu.make_async_remote_copy(
            src_ref=major_ref.at[app], dst_ref=other_ref.at[app],
            send_sem=flip_send.at[app], recv_sem=flip_recv.at[app],
            device_id=(dom, 1 - spin), device_id_type=MESH)

    def edge_copies(n, first, rows):
        part = pl.ds(first, rows)
        tail = pltpu.make_async_remote_copy(
            src_ref=split_ref.at[pl.ds(blocks - RANGE, RANGE), part],
            dst_ref=edge_ref.at[pl.ds(0, RANGE), part],
            send_sem=edge_send.at[n, 0], recv_sem=edge_recv.at[n, 0],
            device_id=(right, spin), device_id_type=MESH)
        head = pltpu.make_async_remote_copy(
            src_ref=split_ref.at[pl.ds(0, RANGE), part],
            dst_ref=edge_ref.at[pl.ds(RANGE, RANGE), part],
            send_sem=edge_send.at[n, 1], recv_sem=edge_recv.at[n, 1],
            device_id=(left, spin), device_id_type=MESH)
        return tail, head

    def to_major(value, scratch, base, store):
        for b, piece in enumerate(value):
            scratch[pl.ds(base + b * vecs, vecs), :] = piece
        for k in range(vecs):
            store(k, scratch[pl.ds(base + k, CHUNK, stride=vecs), :].astype(BF16))

    def tree(parts):
        while len(parts) > 1:
            parts = [sum(parts[p + 1:p + 2], parts[p]) for p in range(0, len(parts), 2)]
        return parts[0]

    def stage(n, ref, send, recv, rank, size, peer):
        def copy(shift, slot):
            return pltpu.make_async_remote_copy(
                src_ref=ref.at[n, rank], dst_ref=ref.at[n, slot],
                send_sem=send.at[n, shift], recv_sem=recv.at[n, slot],
                device_id=peer(shift), device_id_type=MESH)

        def begin(value):
            ref[n, rank] = value
            for shift in range(1, size):
                copy(shift, rank).start()

        def end():
            for shift in range(1, size):
                copy(shift, (rank + size - shift) % size).wait_recv()
            for shift in range(1, size):
                copy(shift, rank).wait_send()
            return tree([ref[n, slot] for slot in range(size)])
        return begin, end

    def staged(n):
        begin_a, end_a = stage(n, stage_a_ref, a_send, a_recv, rank_a, group_size, peer_a)
        begin_b, end_b = stage(n, stage_b_ref, b_send, b_recv, rank_b, groups, peer_b)
        return begin_a, lambda: begin_b(end_a()), end_b

    def share(n, ref, value, size, work):
        if not direct:
            begin, middle, end = staged(n)
            begin(value)
            done = work()
            middle()
            return end() * (1.0 / norm), done
        per = width // size
        rows = -(-vecs // per)
        out = value
        for q in range(1, per):
            moved = pltpu.roll(pltpu.roll(value, (-q * rows) % vecs, 0), q * size, 1)
            out = jnp.where((lane >= q * size) & (lane < (q + 1) * size), moved, out)
        me = dom * 2 + spin
        ref[me] = out[:rows]
        for target in everyone():
            pltpu.make_async_remote_copy(
                src_ref=ref.at[me], dst_ref=ref.at[me],
                send_sem=all_send.at[n], recv_sem=all_recv.at[n],
                device_id=target, device_id_type=MESH).start()
        done = work()
        others = ref.at[pl.ds(0, devices - 1)]
        whole = pltpu.make_async_remote_copy(
            src_ref=others, dst_ref=others, send_sem=all_send.at[n], recv_sem=all_recv.at[n],
            device_id=(dom, 1 - spin), device_id_type=MESH)
        whole.wait_recv()
        whole.wait_send()
        fold_ref[pl.ds(0, rows), :] = tree([ref[slot] for slot in range(devices)])
        total = fold_ref[...] * (1.0 / norm)
        out = jnp.where((lane < size) & (row < rows), total, 0.0)
        for q in range(1, per):
            moved = pltpu.roll(pltpu.roll(total, (q * rows) % vecs, 0), width - q * size, 1)
            out = jnp.where((lane < size) & (row >= q * rows) & (row < (q + 1) * rows), moved, out)
        return out, done

    def lanes(value, start, size):
        moved = value if start == 0 else pltpu.roll(value, width - start, 1)
        return jnp.where(lane < size, moved, 0.0)

    def tall(pieces):
        pad = width - vecs * len(pieces)
        return jnp.concatenate(list(pieces) + [jnp.zeros((pad, width), F32)], axis=0)

    def folded(value):
        wide = value.shape[1]
        fold_ref[:, pl.ds(0, wide)] = value[:vecs] + value[vecs:]
        both = fold_ref[...]
        both = both + pltpu.roll(both, width - vecs, 1)
        out = jnp.where(lane < vecs, both, 0.0)
        for g in range(1, wide // pair):
            inside = (lane >= vecs * g) & (lane < vecs * (g + 1))
            out = jnp.where(inside, pltpu.roll(both, width - vecs * g, 1), out)
        return out

    def wide_rows(ref, first, rows, tiles):
        return jnp.concatenate([ref[tile, pl.ds(first, rows), :] for tile in tiles], axis=1)

    def gram(first, rows, size, tiles):
        return dot(
            wide_rows(split_ref, first, rows, tiles), wide_rows(split_ref, 0, size, tiles), NT)

    def prepare(span_gram, count):
        eye = jnp.where(wide_row == wide_lane, 1.0, 0.0)
        once = 2.0 * eye - span_gram
        left_over = high_dot(eye - span_gram, eye - span_gram, NN)
        square = once + high_dot(left_over, once, NN)
        for n, table in enumerate([once, square, left_over][:count]):
            high, low = halves(table)
            weight_ref[n, :, pl.ds(0, width)] = high
            weight_ref[n, :, pl.ds(width, width)] = low

    def factor(first_t, image_gram, span_count, count):
        first = split(first_t)
        mixed = []
        for n in range(count):
            out = dot(first, weight_ref[n], NN)
            out = out[:vecs] + out[vecs:]
            mixed.append(out[:, :width] + out[:, width:])
        total_t = mixed[0]
        out = dot(split(mixed[1]), first, NT)
        fold_ref[:, pl.ds(0, pair)] = out[:vecs] + out[vecs:]
        both = fold_ref[...]
        square = image_gram - both - pltpu.roll(both, width - vecs, 1)
        table = jnp.where(lane < vecs, square, jnp.where(lane == row + vecs, 1.0, 0.0))
        table = table - pltpu.roll(total_t, pair, 1)
        if count > 2:
            table = table + pltpu.roll(mixed[2], pair + span_count, 1)
        lower = jnp.zeros((vecs, width), F32)
        for j in range(vecs):
            column = jnp.broadcast_to(table[:, j:j + 1], (vecs, width))
            pivot_row = jnp.broadcast_to(table[j:j + 1, :], (vecs, width))
            pivot = jnp.broadcast_to(column[j:j + 1, :], (vecs, width))
            scale = lax.rsqrt(pivot)
            column = column * scale
            lower = jnp.where((lane == j) & (row >= j), column, lower)
            pivot_row = pivot_row * scale
            table = jnp.where(
                row == j, pivot_row, jnp.where(row > j, table - column * pivot_row, table))
        mixer = jnp.zeros((vecs, width), F32)
        for g in range(span_count // vecs + 1):
            source = pair + vecs * g if g < span_count // vecs else vecs
            moved = pltpu.roll(table, (pair * g - source) % width, 1)
            mixer = jnp.where((lane >= pair * g) & (lane < pair * g + vecs), moved, mixer)
        mixer = mixer + pltpu.roll(mixer, vecs, 1)
        low = mixer - mixer.astype(BF16).astype(F32)
        return (
            total_t + pltpu.roll(lower, span_count, 1), jnp.concatenate([mixer, low], axis=0), table)

    def split_products(out, k, base, half_size, size, ref):
        high, low = halves(out)
        ref[k, pl.ds(base, size), :] = high
        ref[k, pl.ds(half_size + base, size), :] = low

    def products(app):
        def body(two, carry):
            weights = hop_ref[pl.ds(pl.multiple_of(two * 2 * width, 2 * width), 2 * width), :]
            for k in range(vecs):
                out = dot(major_ref[app, k], weights, NT)
                for half in range(2):
                    at = pl.multiple_of((two * 2 + half) * blocks, blocks)
                    split_products(
                        out[:, half * width:(half + 1) * width], k, at, kinds * blocks, blocks,
                        prod_ref)
            return carry
        lax.fori_loop(0, types // 2, body, 0)

    def flip_products(app):
        for k in range(vecs):
            out = dot(other_ref[app, k], soc_ref[spin], NT)
            split_products(out, k, types * blocks, kinds * blocks, blocks, prod_ref)

    def gather():
        def body(two, carry):
            chosen = jnp.concatenate([select_ref[n % kinds] for n in range(2 * kinds)], axis=1)
            held = jnp.concatenate([prod_ref[2 * two], prod_ref[2 * two + 1]], axis=1)
            out = dot(chosen, held, NN)
            for half in range(2):
                for i in range(blocks // vecs):
                    block_ref[pl.ds(i * vecs * vecs + 2 * two + half, vecs, stride=vecs), :] = (
                        out[i * vecs:(i + 1) * vecs, half * width:(half + 1) * width])
            return carry
        lax.fori_loop(0, vecs // 2, body, 0)

    def edge_gather():
        reach = 2 * RANGE
        source = far_ref[...].reshape(vecs * reach, width)

        for two in range(types // 2):
            out = dot(source, hop_ref[pl.ds(two * 2 * width, 2 * width), :], NT)
            for half in range(2):
                for k in range(vecs):
                    split_products(
                        out[k * reach:(k + 1) * reach, half * width:(half + 1) * width], k,
                        (two * 2 + half) * reach, types * reach, reach, edge_prod_ref)
        chosen = jnp.concatenate([edge_select_ref[...]] * 2, axis=1)
        for two in range(vecs // 2):
            held = jnp.concatenate([edge_prod_ref[2 * two], edge_prod_ref[2 * two + 1]], axis=1)
            out = dot(chosen, held, NN)
            for half in range(2):
                for end, base in enumerate((0, (blocks - RANGE) * vecs)):
                    at = pl.ds(base + 2 * two + half, RANGE, stride=vecs)
                    block_ref[at, :] = block_ref[at, :] + out[
                        end * RANGE:(end + 1) * RANGE, half * width:(half + 1) * width]

    def assemble(field_ref, first, low, high):
        def body(block, carry):
            image = pot_ref[pl.ds(0, 1), cols(block)] * field_ref[:, cols(block)]
            at = pl.multiple_of(block * vecs, vecs)
            image = image + block_ref[pl.ds(at, vecs), :]
            split_ref[block, pl.ds(first, pair), :] = split(image)
            return carry
        lax.fori_loop(low, high, body, 0, unroll=8)

    def chunk_pieces(value):
        return [value[:, b * width:(b + 1) * width] for b in range(CHUNK)]

    def store_major(app, chunk):
        def store(k, rounded):
            major_ref[app, k, pl.ds(pl.multiple_of(chunk * CHUNK, CHUNK), CHUNK), :] = rounded
        return store

    def round_body(chunk, carry):
        pieces = chunk_pieces(vec_ref[:, cols(chunk * CHUNK, CHUNK)])
        for b, piece in enumerate(pieces):
            split_ref[chunk * CHUNK + b, pl.ds(2 * kept, pair), :] = split(piece)
        to_major(pieces, block_ref, chunk * CHUNK * vecs, store_major(0, chunk))
        return carry

    def store_far(k, rounded):
        far_ref[k] = rounded

    wide_row = lax.broadcasted_iota(I32, (width, width), 0)
    wide_lane = lax.broadcasted_iota(I32, (width, width), 1)
    chunks = blocks // CHUNK
    loads[0].wait()
    round_body(0, 0)
    round_body(chunks - 1, 0)
    pl.semaphore_wait(barrier, len(greeted))
    vec_edges = edge_copies(0, 2 * kept, pair)
    for copy in vec_edges:
        copy.start()
    lax.fori_loop(1, chunks - 1, round_body, 0)
    flip_one = flip_copy(0)
    flip_one.start()
    for copy in loads[1:5]:
        copy.wait()

    local = lax.broadcasted_iota(I32, (slots, blocks), 1)
    slot_at = lax.broadcasted_iota(I32, (slots, blocks), 0)
    shift = nbr_ref[...] - (dom * blocks + local) + RANGE
    total = dom_total * blocks
    shift = jnp.where(shift < 0, shift + total, shift)
    shift = jnp.where(shift >= total, shift - total, shift)
    place = local + shift - RANGE
    live = slot_at < count_ref[...]
    inside = (place >= 0) & (place < blocks)
    code = jnp.where(live & inside, type_ref[...] * STRIDE + shift, -1)
    edge_code = jnp.where(place < 0, place + RANGE, place - blocks + RANGE)
    edge_code = jnp.where(live & ~inside, type_ref[...] * (2 * RANGE) + edge_code, -1)

    def counts(codes, base):
        wanted = row + base
        return tree([jnp.where(codes[s:s + 1, :] == wanted, 1.0, 0.0) for s in range(slots)])

    band = (wide_lane - wide_row <= RANGE) & (wide_row - wide_lane <= RANGE)
    per_tile = width // STRIDE
    blank = jnp.zeros((vecs, width), F32)
    for tile in range(types // per_tile):
        pieces = []
        for r in range(width // vecs):
            live_rows = (r * vecs) % STRIDE <= 2 * RANGE
            pieces.append(counts(code, tile * width + r * vecs) if live_rows else blank)
        table = jnp.concatenate(pieces, axis=0).T
        for t in range(per_tile):
            moved = pltpu.roll(
                table, (-RANGE - STRIDE * t) % width, 1, stride=1, stride_axis=0)
            select_ref[tile * per_tile + t] = jnp.where(band, moved, 0.0).astype(BF16)
    flip_local = fliploc_ref[...] - dom * blocks
    select_ref[types] = jnp.where(flip_local == wide_row, 1.0, 0.0).T.astype(BF16)
    table = jnp.concatenate(
        [counts(edge_code, r * vecs) for r in range(width // vecs)], axis=0).T
    edge_select_ref[...] = jnp.concatenate(
        [table[:RANGE], table[blocks - RANGE:]], axis=0).astype(BF16)
    fold_ref[...] = jnp.zeros((vecs, width), F32)

    loads[5].wait()

    def split_basis(chunk, carry):
        for b in range(4):
            block = chunk * 4 + b
            for g in range(kept_groups):
                split_ref[block, pl.ds(g * pair, pair), :] = split(
                    basis_ref[pl.ds(g * vecs, vecs), cols(block)])
        return carry
    lax.fori_loop(0, blocks // 4, split_basis, 0, unroll=2)
    basis_edges = edge_copies(1, 0, 2 * kept)
    for copy in basis_edges:
        copy.start()
    low_gram = gram(0, rows_one, rows_one, range(blocks))
    packed_low = jnp.zeros((vecs, width), F32)
    for g in range(span_one // vecs):
        piece = folded(low_gram[g * pair:(g + 1) * pair])
        packed_low = packed_low + (pltpu.roll(piece, g * span_one, 1) if g else piece)
    low_begin, low_middle, low_end = staged(0)
    low_begin(packed_low)
    for copy in loads[6:]:
        copy.wait()

    products(0)
    low_middle()
    flip_one.wait_recv()
    flip_products(0)
    gather()
    assemble(vec_ref, rows_one, RANGE, blocks - RANGE)
    result = gram(rows_one, pair, rows_two, range(RANGE, blocks - RANGE))
    for copy in vec_edges:
        copy.wait_recv()
    to_major(
        [edge_ref[b, pl.ds(2 * kept, pair), :].astype(F32)[:vecs] for b in range(2 * RANGE)],
        near_ref, 0, store_far)
    edge_gather()
    assemble(vec_ref, rows_one, 0, RANGE)
    assemble(vec_ref, rows_one, blocks - RANGE, blocks)
    image_edges = edge_copies(2, rows_one, pair)
    ends = list(range(RANGE)) + list(range(blocks - RANGE, blocks))
    result = folded(result + gram(rows_one, pair, rows_two, ends))

    def while_sharing():
        for copy in image_edges:
            copy.start()
        packed = low_end() * (1.0 / norm)
        span_gram = tall(
            [lanes(packed, g * span_one, span_one) for g in range(span_one // vecs)])
        prepare(span_gram, 3)
        return span_gram
    packed, span_gram = share(1, all_one_ref, result, span_one + vecs, while_sharing)
    coefs, mixer, table = factor(
        lanes(packed, 0, span_one), lanes(packed, span_one, vecs), span_one, 3)
    small_ref[pl.ds(0, vecs), :] = coefs
    mixer = mixer.astype(BF16)[:, :rows_two]
    for copy in image_edges:
        copy.wait_send()

    def mix_body(chunk, carry):
        out = dot(
            mixer, wide_rows(split_ref, 0, rows_two, [chunk * CHUNK + b for b in range(CHUNK)]), NN)
        value = out[:vecs] + out[vecs:]
        one_ref[:, cols(chunk * CHUNK, CHUNK)] = value
        pieces = chunk_pieces(value)
        for b, piece in enumerate(pieces):
            split_ref[chunk * CHUNK + b, pl.ds(rows_one, pair), :] = split(piece)
        to_major(pieces, block_ref, chunk * CHUNK * vecs, store_major(1, chunk))
        return carry
    lax.fori_loop(0, chunks, mix_body, 0)
    flip_two = flip_copy(1)
    flip_two.start()
    products(1)
    for copy in image_edges + basis_edges:
        copy.wait_recv()
    out = dot(mixer, wide_rows(edge_ref, 0, rows_two, range(2 * RANGE)), NN)
    to_major(chunk_pieces(out[:vecs] + out[vecs:]), near_ref, 0, store_far)
    flip_two.wait_recv()
    flip_products(1)
    gather()
    edge_gather()
    assemble(one_ref, rows_two, 0, blocks)
    result = folded(gram(rows_two, pair, rows_two + pair, range(blocks)))

    def while_sharing_two():
        cross = lanes(table, pair + span_one, span_one)
        cross = cross + jnp.where(lane == row + span_one, 1.0, 0.0)
        low = jnp.concatenate(
            [jnp.zeros((span_one, width), F32), cross,
             jnp.zeros((width - span_two, width), F32)], axis=0)
        prepare(span_gram + low + jnp.where(
            (wide_row < span_one) & (wide_lane >= span_one), low.T, 0.0), 2)
        for copy in vec_edges + basis_edges:
            copy.wait_send()
        flip_one.wait_send()
        flip_two.wait_send()
    packed, _ = share(2, all_two_ref, result, span_two + vecs, while_sharing_two)
    coefs, mixer, _ = factor(
        lanes(packed, 0, span_two), lanes(packed, span_two, vecs), span_two, 2)
    small_ref[pl.ds(vecs, vecs), :] = coefs
    small_ref[pl.ds(pair, pair), :] = mixer


def finish(
    cfg, small_ref, split_ref, one_ref,
    one_hbm, two_hbm, coef_one_hbm, coef_two_hbm,
    two_ref, cut_one_ref, cut_two_ref, store_sem,
):
    _, _, blocks, width, _, _, vecs, kept, _, _ = cfg
    span_one = kept + vecs
    span_two = span_one + vecs
    pieces = 8
    size = blocks // pieces * width
    stores = [pltpu.make_async_copy(one_ref, one_hbm.at[0], store_sem.at[0])]
    stores[-1].start()
    mixer = small_ref[pl.ds(2 * vecs, 2 * vecs), :].astype(BF16)[:, :2 * (span_two + vecs)]
    for piece in range(pieces):
        part = pl.ds(piece * size, size)
        tiles = range(piece * (blocks // pieces), (piece + 1) * (blocks // pieces))
        out = dot(mixer, jnp.concatenate([split_ref[tile] for tile in tiles], axis=1), NN)
        two_ref[:, part] = out[:vecs] + out[vecs:]
        stores.append(pltpu.make_async_copy(
            two_ref.at[:, part], two_hbm.at[0, :, part], store_sem.at[1 + piece]))
        stores[-1].start()
    cut_one_ref[...] = small_ref[pl.ds(0, vecs), :span_one + vecs]
    cut_two_ref[...] = small_ref[pl.ds(vecs, vecs), :span_two + vecs]
    stores.append(pltpu.make_async_copy(cut_one_ref, coef_one_hbm, store_sem.at[1 + pieces]))
    stores.append(pltpu.make_async_copy(cut_two_ref, coef_two_hbm, store_sem.at[2 + pieces]))
    for copy in stores[-2:]:
        copy.start()
    for copy in stores:
        copy.wait()


def per_device(
    vectors, basis, potential, hop_table, soc_table, nbr_block, nbr_type, nbr_count, flip_block
):
    blocks, slots = nbr_block.shape
    types, width, _ = hop_table.shape
    vecs, kept = vectors.shape[1], basis.shape[1]
    dom_total = lax.axis_size("dom")
    group_doms = 4 if dom_total % 4 == 0 else 1
    groups = dom_total // group_doms
    norm = float(2 * blocks * width * dom_total)
    direct = dom_total <= 32
    cfg = (dom_total, group_doms, blocks, width, types, slots, vecs, kept, norm, direct)
    count = blocks * width
    pair = 2 * vecs
    span_one, span_two = kept + vecs, kept + 2 * vecs
    kinds = types + 1
    seats = 2 * dom_total if direct else 1
    row_count = lambda size: -(-vecs // (width // size))
    vmem = pl.BlockSpec(memory_space=pltpu.VMEM)
    hbm = pl.BlockSpec(memory_space=pltpu.HBM)
    dma = pltpu.SemaphoreType.DMA
    shape = jax.ShapeDtypeStruct
    one, parts, small = pl.pallas_call(
        functools.partial(kernel, cfg),
        name="krylov",
        out_shape=(
            pltpu.VMEM((vecs, count), F32),
            pltpu.VMEM((blocks, 2 * (span_two + vecs), width), BF16),
            pltpu.VMEM((4 * vecs, width), F32),
        ),
        in_specs=[hbm] * 9,
        out_specs=(vmem, vmem, vmem),
        scratch_shapes=[
            pltpu.VMEM((vecs, count), F32),
            pltpu.VMEM((kept, count), F32),
            pltpu.VMEM((1, count), F32),
            pltpu.VMEM((types * width, width), BF16),
            pltpu.VMEM(soc_table.shape, BF16),
            pltpu.VMEM((slots, blocks), I32),
            pltpu.VMEM((slots, blocks), I32),
            pltpu.VMEM((1, blocks), I32),
            pltpu.VMEM((1, blocks), I32),
            pltpu.VMEM((blocks * vecs, width), F32),
            pltpu.VMEM((2 * RANGE, 2 * span_two, width), BF16),
            pltpu.VMEM((2, vecs, blocks, width), BF16),
            pltpu.VMEM((2, vecs, blocks, width), BF16),
            pltpu.VMEM((2 * RANGE * vecs, width), F32),
            pltpu.VMEM((vecs, 2 * RANGE, width), BF16),
            pltpu.VMEM((vecs, 2 * kinds * blocks, width), BF16),
            pltpu.VMEM((vecs, 4 * RANGE * types, width), BF16),
            pltpu.VMEM((kinds, blocks, width), BF16),
            pltpu.VMEM((2 * RANGE, 2 * RANGE * types), BF16),
            pltpu.VMEM((vecs, width), F32),
            pltpu.VMEM((3, width, 2 * width), BF16),
            pltpu.VMEM((3, 2 * group_doms, vecs, width), F32),
            pltpu.VMEM((3, groups, vecs, width), F32),
            pltpu.VMEM((seats, row_count(span_one + vecs), width), F32),
            pltpu.VMEM((seats, row_count(span_two + vecs), width), F32),
            dma((9,)),
            dma((2,)), dma((2,)),
            dma((3, 2)), dma((3, 2)),
            dma((3, 2 * group_doms)), dma((3, 2 * group_doms)),
            dma((3, groups)), dma((3, groups)),
            dma((3,)), dma((3,)),
        ],
        compiler_params=pltpu.CompilerParams(
            collective_id=0, has_side_effects=True, vmem_limit_bytes=32 * 1024 * 1024),
    )(*[pltpu.with_memory_space_constraint(value, pltpu.HBM) for value in (
        vectors, basis, potential, hop_table.reshape(types * width, width), soc_table,
        nbr_block.T, nbr_type.T, nbr_count.reshape(1, blocks), flip_block.reshape(1, blocks))])
    one, two, coef_one, coef_two = pl.pallas_call(
        functools.partial(finish, cfg),
        name="finish",
        out_shape=(
            shape((1, vecs, count), F32),
            shape((1, vecs, count), F32),
            shape((vecs, span_one + vecs), F32),
            shape((vecs, span_two + vecs), F32),
        ),
        in_specs=[vmem, vmem, vmem],
        out_specs=(hbm,) * 4,
        scratch_shapes=[
            pltpu.VMEM((vecs, count), F32),
            pltpu.VMEM((vecs, span_one + vecs), F32),
            pltpu.VMEM((vecs, span_two + vecs), F32),
            dma((11,)),
        ],
        compiler_params=pltpu.CompilerParams(vmem_limit_bytes=16 * 1024 * 1024),
    )(small, parts, one)
    return one, two, coef_one.T, coef_two.T


def solution(mesh):
    return jax.shard_map(
        per_device,
        mesh=mesh,
        in_specs=(
            P("spin", None, "dom"),
            P("spin", None, "dom"),
            P("spin", "dom"),
            P(),
            P(),
            P("dom", None),
            P("dom", None),
            P("dom"),
            P("dom"),
        ),
        out_specs=(P("spin", None, "dom"), P("spin", None, "dom"), P(), P()),
        check_vma=False,
    )
```

time: 40.2 us -> 38.2 us (0.950)
  Pallas kernels: 39.4 us -> 37.4 us
    pallas_call x1, Pallas kernels: 38.2 us -> 36.2 us  [per_device(): pl.pallas_call(functools.partial(kernel, cfg), name='krylov', out_shape=(...]
where the time goes in v3:
time: 38.2 us; the launch traced here: 38 us
  Pallas kernels  37.4 us (98%)
  between operations  0.64 us (2%)
    pallas_call x1, Pallas kernels, per_device(): pl.pallas_call(functools.partial(kernel, cfg), name='krylov', out_shape=(...  36.2 us
    pallas_call x1, Pallas kernels, per_device(): pl.pallas_call(functools.partial(finish, cfg), name='finish', out_shape=(...  1.2 us

profile of v3, /device:TPU:0, one launch (start us, length us, event | category | flops | bytes accessed | tf_op | source)
XLA Modules:
  0.0 38.0 jit_solution(15918821411120729706)
XLA Ops:
  0.6 36.2 %krylov.1 = (f32[8,16384]{1,0:T(8,128)S(1)}, bf16[128,80,128]{2,1,0:T(8,128)(2,1)S(1)}, f32[32,128]{1,0:T(8,128)S(1)}) custom-call(f32[1,8,16384]{2,1,0:T(8,128)} %vec_hbm.1, f32[1,16,16384]{2,1,0:T(8,128)} %basis_hbm.1, f32[1,16384]{1,0:T(1,128)} %pot_hbm.1, bf16[1024,128]{1,0:T(8,128)(2,1)} %bitcast.7, bf16[2,128,128]{2,1,0:T(8,128)(2,1)} %soc_hbm.1, ...), custom_call_target="tpu_custom_call" | custom-call | tf_op jit(solution)/shard_map/krylov/pallas_call | solution.py:564
  36.8 1.2 %finish.1 = (f32[1,8,16384]{2,1,0:T(8,128)}, f32[1,8,16384]{2,1,0:T(8,128)}, f32[8,32]{1,0:T(8,128)}, f32[8,40]{1,0:T(8,128)}) custom-call(f32[32,128]{1,0:T(8,128)S(1)} %get-tuple-element.11.small_ref, bf16[128,80,128]{2,1,0:T(8,128)(2,1)S(1)} %get-tuple-element.12.split_ref, f32[8,16384]{1,0:T(8,128)S(1)} %get-tuple-element.13.one_ref), custom_call_target="tpu_custom_call" | custom-call | tf_op jit(solution)/shard_map/finish/pallas_call | solution.py:612

commit v4 on v3

--- a/solution.py
+++ b/solution.py
@@ -42,7 +42,7 @@
     vec_ref, basis_ref, pot_ref, hop_ref, soc_ref, nbr_ref, type_ref, count_ref, fliploc_ref,
     block_ref, edge_ref, major_ref, other_ref, near_ref, far_ref, prod_ref, edge_prod_ref,
     select_ref, edge_select_ref, fold_ref, weight_ref, stage_a_ref, stage_b_ref,
-    all_one_ref, all_two_ref,
+    all_low_ref, all_one_ref, all_two_ref,
     load_sem, flip_send, flip_recv, edge_send, edge_recv, a_send, a_recv, b_send, b_recv,
     all_send, all_recv,
 ):
@@ -161,9 +161,32 @@
         begin_b, end_b = stage(n, stage_b_ref, b_send, b_recv, rank_b, groups, peer_b)
         return begin_a, lambda: begin_b(end_a()), end_b
 
+    def exchange(n, ref):
+        if not direct:
+            return staged(n)
+        me = dom * 2 + spin
+
+        def begin(value):
+            ref[me] = value
+            for target in everyone():
+                pltpu.make_async_remote_copy(
+                    src_ref=ref.at[me], dst_ref=ref.at[me],
+                    send_sem=all_send.at[n], recv_sem=all_recv.at[n],
+                    device_id=target, device_id_type=MESH).start()
+
+        def end():
+            others = ref.at[pl.ds(0, devices - 1)]
+            whole = pltpu.make_async_remote_copy(
+                src_ref=others, dst_ref=others, send_sem=all_send.at[n], recv_sem=all_recv.at[n],
+                device_id=(dom, 1 - spin), device_id_type=MESH)
+            whole.wait_recv()
+            whole.wait_send()
+            return tree([ref[slot] for slot in range(devices)])
+        return begin, lambda: None, end
+
     def share(n, ref, value, size, work):
+        begin, middle, end = exchange(n, ref)
         if not direct:
-            begin, middle, end = staged(n)
             begin(value)
             done = work()
             middle()
@@ -174,21 +197,9 @@
         for q in range(1, per):
             moved = pltpu.roll(pltpu.roll(value, (-q * rows) % vecs, 0), q * size, 1)
             out = jnp.where((lane >= q * size) & (lane < (q + 1) * size), moved, out)
-        me = dom * 2 + spin
-        ref[me] = out[:rows]
-        for target in everyone():
-            pltpu.make_async_remote_copy(
-                src_ref=ref.at[me], dst_ref=ref.at[me],
-                send_sem=all_send.at[n], recv_sem=all_recv.at[n],
-                device_id=target, device_id_type=MESH).start()
+        begin(out[:rows])
         done = work()
-        others = ref.at[pl.ds(0, devices - 1)]
-        whole = pltpu.make_async_remote_copy(
-            src_ref=others, dst_ref=others, send_sem=all_send.at[n], recv_sem=all_recv.at[n],
-            device_id=(dom, 1 - spin), device_id_type=MESH)
-        whole.wait_recv()
-        whole.wait_send()
-        fold_ref[pl.ds(0, rows), :] = tree([ref[slot] for slot in range(devices)])
+        fold_ref[pl.ds(0, rows), :] = end()
         total = fold_ref[...] * (1.0 / norm)
         out = jnp.where((lane < size) & (row < rows), total, 0.0)
         for q in range(1, per):
@@ -285,7 +296,7 @@
                         out[:, half * width:(half + 1) * width], k, at, kinds * blocks, blocks,
                         prod_ref)
             return carry
-        lax.fori_loop(0, types // 2, body, 0)
+        lax.fori_loop(0, types // 2, body, 0, unroll=2)
 
     def flip_products(app):
         for k in range(vecs):
@@ -302,7 +313,7 @@
                     block_ref[pl.ds(i * vecs * vecs + 2 * two + half, vecs, stride=vecs), :] = (
                         out[i * vecs:(i + 1) * vecs, half * width:(half + 1) * width])
             return carry
-        lax.fori_loop(0, vecs // 2, body, 0)
+        lax.fori_loop(0, vecs // 2, body, 0, unroll=2)
 
     def edge_gather():
         reach = 2 * RANGE
@@ -424,7 +435,7 @@
     for g in range(span_one // vecs):
         piece = folded(low_gram[g * pair:(g + 1) * pair])
         packed_low = packed_low + (pltpu.roll(piece, g * span_one, 1) if g else piece)
-    low_begin, low_middle, low_end = staged(0)
+    low_begin, low_middle, low_end = exchange(0, all_low_ref)
     low_begin(packed_low)
     for copy in loads[6:]:
         copy.wait()
@@ -474,7 +485,7 @@
             split_ref[chunk * CHUNK + b, pl.ds(rows_one, pair), :] = split(piece)
         to_major(pieces, block_ref, chunk * CHUNK * vecs, store_major(1, chunk))
         return carry
-    lax.fori_loop(0, chunks, mix_body, 0)
+    lax.fori_loop(0, chunks, mix_body, 0, unroll=2)
     flip_two = flip_copy(1)
     flip_two.start()
     products(1)
@@ -595,6 +606,7 @@
             pltpu.VMEM((3, width, 2 * width), BF16),
             pltpu.VMEM((3, 2 * group_doms, vecs, width), F32),
             pltpu.VMEM((3, groups, vecs, width), F32),
+            pltpu.VMEM((seats, vecs, width), F32),
             pltpu.VMEM((seats, row_count(span_one + vecs), width), F32),
             pltpu.VMEM((seats, row_count(span_two + vecs), width), F32),
             dma((9,)),

time: 38.2 us -> 33.9 us (0.89)
  Pallas kernels: 37.4 us -> 33.1 us
    pallas_call x1, Pallas kernels: 36.2 us -> 31.9 us  [per_device(): pl.pallas_call(functools.partial(kernel, cfg), name='krylov', out_shape=(...]
where the time goes in v4:
time: 33.9 us; the launch traced here: 33.8 us
  Pallas kernels  33.1 us (98%)
  between operations  0.64 us (2%)
    pallas_call x1, Pallas kernels, per_device(): pl.pallas_call(functools.partial(kernel, cfg), name='krylov', out_shape=(...  31.9 us
    pallas_call x1, Pallas kernels, per_device(): pl.pallas_call(functools.partial(finish, cfg), name='finish', out_shape=(...  1.2 us

profile of v4, /device:TPU:0, one launch (start us, length us, event | category | flops | bytes accessed | tf_op | source)
XLA Modules:
  0.0 33.8 jit_solution(5332406489373727780)
XLA Ops:
  0.6 31.9 %krylov.1 = (f32[8,16384]{1,0:T(8,128)S(1)}, bf16[128,80,128]{2,1,0:T(8,128)(2,1)S(1)}, f32[32,128]{1,0:T(8,128)S(1)}) custom-call(f32[1,8,16384]{2,1,0:T(8,128)} %vec_hbm.1, f32[1,16,16384]{2,1,0:T(8,128)} %basis_hbm.1, f32[1,16384]{1,0:T(1,128)} %pot_hbm.1, bf16[1024,128]{1,0:T(8,128)(2,1)} %bitcast.7, bf16[2,128,128]{2,1,0:T(8,128)(2,1)} %soc_hbm.1, ...), custom_call_target="tpu_custom_call" | custom-call | tf_op jit(solution)/shard_map/krylov/pallas_call | solution.py:575
  32.6 1.2 %finish.1 = (f32[1,8,16384]{2,1,0:T(8,128)}, f32[1,8,16384]{2,1,0:T(8,128)}, f32[8,32]{1,0:T(8,128)}, f32[8,40]{1,0:T(8,128)}) custom-call(f32[32,128]{1,0:T(8,128)S(1)} %get-tuple-element.11.small_ref, bf16[128,80,128]{2,1,0:T(8,128)(2,1)S(1)} %get-tuple-element.12.split_ref, f32[8,16384]{1,0:T(8,128)S(1)} %get-tuple-element.13.one_ref), custom_call_target="tpu_custom_call" | custom-call | tf_op jit(solution)/shard_map/finish/pallas_call | solution.py:624

commit v5 on v4

--- a/solution.py
+++ b/solution.py
@@ -41,7 +41,7 @@
     one_ref, split_ref, small_ref,
     vec_ref, basis_ref, pot_ref, hop_ref, soc_ref, nbr_ref, type_ref, count_ref, fliploc_ref,
     block_ref, edge_ref, major_ref, other_ref, near_ref, far_ref, prod_ref, edge_prod_ref,
-    select_ref, edge_select_ref, fold_ref, weight_ref, stage_a_ref, stage_b_ref,
+    select_ref, edge_select_ref, fold_ref, inner_ref, weight_ref, stage_a_ref, stage_b_ref,
     all_low_ref, all_one_ref, all_two_ref,
     load_sem, flip_send, flip_recv, edge_send, edge_recv, a_send, a_recv, b_send, b_recv,
     all_send, all_recv,
@@ -230,8 +230,11 @@
         return jnp.concatenate([ref[tile, pl.ds(first, rows), :] for tile in tiles], axis=1)
 
     def gram(first, rows, size, tiles):
-        return dot(
-            wide_rows(split_ref, first, rows, tiles), wide_rows(split_ref, 0, size, tiles), NT)
+        tiles = list(tiles)
+        middle = len(tiles) // 2
+        return sum(
+            dot(wide_rows(split_ref, first, rows, part), wide_rows(split_ref, 0, size, part), NT)
+            for part in (tiles[:middle], tiles[middle:]))
 
     def prepare(span_gram, count):
         eye = jnp.where(wide_row == wide_lane, 1.0, 0.0)
@@ -446,7 +449,7 @@
     flip_products(0)
     gather()
     assemble(vec_ref, rows_one, RANGE, blocks - RANGE)
-    result = gram(rows_one, pair, rows_two, range(RANGE, blocks - RANGE))
+    inner_ref[...] = gram(rows_one, pair, rows_two, range(RANGE, blocks - RANGE))
     for copy in vec_edges:
         copy.wait_recv()
     to_major(
@@ -457,7 +460,7 @@
     assemble(vec_ref, rows_one, blocks - RANGE, blocks)
     image_edges = edge_copies(2, rows_one, pair)
     ends = list(range(RANGE)) + list(range(blocks - RANGE, blocks))
-    result = folded(result + gram(rows_one, pair, rows_two, ends))
+    result = folded(inner_ref[...] + gram(rows_one, pair, rows_two, ends))
 
     def while_sharing():
         for copy in image_edges:
@@ -567,6 +570,7 @@
     span_one, span_two = kept + vecs, kept + 2 * vecs
     kinds = types + 1
     seats = 2 * dom_total if direct else 1
+    rounds, near, far = (1, 1, 1) if direct else (3, 2 * group_doms, groups)
     row_count = lambda size: -(-vecs // (width // size))
     vmem = pl.BlockSpec(memory_space=pltpu.VMEM)
     hbm = pl.BlockSpec(memory_space=pltpu.HBM)
@@ -603,17 +607,18 @@
             pltpu.VMEM((kinds, blocks, width), BF16),
             pltpu.VMEM((2 * RANGE, 2 * RANGE * types), BF16),
             pltpu.VMEM((vecs, width), F32),
+            pltpu.VMEM((pair, 2 * span_two), F32),
             pltpu.VMEM((3, width, 2 * width), BF16),
-            pltpu.VMEM((3, 2 * group_doms, vecs, width), F32),
-            pltpu.VMEM((3, groups, vecs, width), F32),
+            pltpu.VMEM((rounds, near, vecs, width), F32),
+            pltpu.VMEM((rounds, far, vecs, width), F32),
             pltpu.VMEM((seats, vecs, width), F32),
             pltpu.VMEM((seats, row_count(span_one + vecs), width), F32),
             pltpu.VMEM((seats, row_count(span_two + vecs), width), F32),
             dma((9,)),
             dma((2,)), dma((2,)),
             dma((3, 2)), dma((3, 2)),
-            dma((3, 2 * group_doms)), dma((3, 2 * group_doms)),
-            dma((3, groups)), dma((3, groups)),
+            dma((rounds, near)), dma((rounds, near)),
+            dma((rounds, far)), dma((rounds, far)),
             dma((3,)), dma((3,)),
         ],
         compiler_params=pltpu.CompilerParams(

time: 33.9 us -> 33.2 us (0.979)
  Pallas kernels: 33.1 us -> 32.4 us
    pallas_call x1, Pallas kernels: 31.9 us -> 31.2 us  [per_device(): pl.pallas_call(functools.partial(kernel, cfg), name='krylov', out_shape=(...]
where the time goes in v5:
time: 33.2 us; the launch traced here: 33.1 us
  Pallas kernels  32.4 us (98%)
  between operations  0.64 us (2%)
    pallas_call x1, Pallas kernels, per_device(): pl.pallas_call(functools.partial(kernel, cfg), name='krylov', out_shape=(...  31.2 us
    pallas_call x1, Pallas kernels, per_device(): pl.pallas_call(functools.partial(finish, cfg), name='finish', out_shape=(...  1.2 us

profile of v5, /device:TPU:0, one launch (start us, length us, event | category | flops | bytes accessed | tf_op | source)
XLA Modules:
  0.0 33.1 jit_solution(9849121105050925216)
XLA Ops:
  0.6 31.2 %krylov.1 = (f32[8,16384]{1,0:T(8,128)S(1)}, bf16[128,80,128]{2,1,0:T(8,128)(2,1)S(1)}, f32[32,128]{1,0:T(8,128)S(1)}) custom-call(f32[1,8,16384]{2,1,0:T(8,128)} %vec_hbm.1, f32[1,16,16384]{2,1,0:T(8,128)} %basis_hbm.1, f32[1,16384]{1,0:T(1,128)} %pot_hbm.1, bf16[1024,128]{1,0:T(8,128)(2,1)} %bitcast.7, bf16[2,128,128]{2,1,0:T(8,128)(2,1)} %soc_hbm.1, ...), custom_call_target="tpu_custom_call" | custom-call | tf_op jit(solution)/shard_map/krylov/pallas_call | solution.py:579
  31.9 1.2 %finish.1 = (f32[1,8,16384]{2,1,0:T(8,128)}, f32[1,8,16384]{2,1,0:T(8,128)}, f32[8,32]{1,0:T(8,128)}, f32[8,40]{1,0:T(8,128)}) custom-call(f32[32,128]{1,0:T(8,128)S(1)} %get-tuple-element.11.small_ref, bf16[128,80,128]{2,1,0:T(8,128)(2,1)S(1)} %get-tuple-element.12.split_ref, f32[8,16384]{1,0:T(8,128)S(1)} %get-tuple-element.13.one_ref), custom_call_target="tpu_custom_call" | custom-call | tf_op jit(solution)/shard_map/finish/pallas_call | solution.py:629

commit v6 on v5

--- a/solution.py
+++ b/solution.py
@@ -231,10 +231,10 @@
 
     def gram(first, rows, size, tiles):
         tiles = list(tiles)
-        middle = len(tiles) // 2
-        return sum(
+        step = max(len(tiles) // 4, 2)
+        return tree([
             dot(wide_rows(split_ref, first, rows, part), wide_rows(split_ref, 0, size, part), NT)
-            for part in (tiles[:middle], tiles[middle:]))
+            for part in (tiles[p:p + step] for p in range(0, len(tiles), step))])
 
     def prepare(span_gram, count):
         eye = jnp.where(wide_row == wide_lane, 1.0, 0.0)
@@ -346,7 +346,7 @@
             image = image + block_ref[pl.ds(at, vecs), :]
             split_ref[block, pl.ds(first, pair), :] = split(image)
             return carry
-        lax.fori_loop(low, high, body, 0, unroll=8)
+        lax.fori_loop(low, high, body, 0, unroll=16 if (high - low) % 16 == 0 else 8)
 
     def chunk_pieces(value):
         return [value[:, b * width:(b + 1) * width] for b in range(CHUNK)]

time: 33.2 us -> 33.1 us (level)
  no operation moved by 1% of the time
where the time goes in v6:
time: 33.1 us; the launch traced here: 32.9 us
  Pallas kernels  32.3 us (98%)
  between operations  0.64 us (2%)
    pallas_call x1, Pallas kernels, per_device(): pl.pallas_call(functools.partial(kernel, cfg), name='krylov', out_shape=(...  31.1 us
    pallas_call x1, Pallas kernels, per_device(): pl.pallas_call(functools.partial(finish, cfg), name='finish', out_shape=(...  1.2 us

profile of v6, /device:TPU:0, one launch (start us, length us, event | category | flops | bytes accessed | tf_op | source)
XLA Modules:
  0.0 32.9 jit_solution(14010701435685561168)
XLA Ops:
  0.6 31.1 %krylov.1 = (f32[8,16384]{1,0:T(8,128)S(1)}, bf16[128,80,128]{2,1,0:T(8,128)(2,1)S(1)}, f32[32,128]{1,0:T(8,128)S(1)}) custom-call(f32[1,8,16384]{2,1,0:T(8,128)} %vec_hbm.1, f32[1,16,16384]{2,1,0:T(8,128)} %basis_hbm.1, f32[1,16384]{1,0:T(1,128)} %pot_hbm.1, bf16[1024,128]{1,0:T(8,128)(2,1)} %bitcast.7, bf16[2,128,128]{2,1,0:T(8,128)(2,1)} %soc_hbm.1, ...), custom_call_target="tpu_custom_call" | custom-call | tf_op jit(solution)/shard_map/krylov/pallas_call | solution.py:579
  31.7 1.2 %finish.1 = (f32[1,8,16384]{2,1,0:T(8,128)}, f32[1,8,16384]{2,1,0:T(8,128)}, f32[8,32]{1,0:T(8,128)}, f32[8,40]{1,0:T(8,128)}) custom-call(f32[32,128]{1,0:T(8,128)S(1)} %get-tuple-element.11.small_ref, bf16[128,80,128]{2,1,0:T(8,128)(2,1)S(1)} %get-tuple-element.12.split_ref, f32[8,16384]{1,0:T(8,128)S(1)} %get-tuple-element.13.one_ref), custom_call_target="tpu_custom_call" | custom-call | tf_op jit(solution)/shard_map/finish/pallas_call | solution.py:629
